TPU v7x, 32 devices: a whole 2x2x4 slice. The times are simulated.
32 devices in a mesh: dp: 4 (over y, x), row: 2 (over core), col: 4 (over z).
Axes of the slice: x: 2, y: 2, z: 4, core: 2. Of those that a mesh axis runs over, the one named last changes fastest.
Arguments:
- inputs: bfloat16 [4096, 1024], P(('dp', 'col'), 'row'), may hold values from -6 to 6
- norm_in: float32 [1, 1024], P(None, 'row'), may hold values from 0.1 to 1.9
- w_proj: bfloat16 [1, 1024, 8, 768], P(None, 'row', 'col'), may hold values from -0.1875 to 0.1875
- w_small: bfloat16 [1, 1024, 8, 2], P(None, 'row', 'col'), may hold values from -0.1875 to 0.1875
- w_conv: float32 [1, 4, 8, 512], P(None, None, 'col'), may hold values from -3 to 3
- a_log: float32 [1, 8], P(None, 'col'), may hold values from -3 to 1.5
- dt_bias: float32 [1, 8], P(None, 'col'), may hold values from -4 to -1
- norm_out: float32 [1, 256], replicated, may hold values from 0.1 to 1.9
- w_out: bfloat16 [1, 8, 256, 1024], P(None, 'col', None, 'row'), may hold values from -0.25 to 0.25
- norm_ffn: float32 [1, 1024], P(None, 'row'), may hold values from 0.1 to 1.9
- w_gu: bfloat16 [1, 1024, 2, 2816], P(None, 'row', None, 'col'), may hold values from -0.1875 to 0.1875
- w_down: bfloat16 [1, 2816, 1024], P(None, 'col', 'row'), may hold values from -0.21875 to 0.21875
- block_resets: int32 [4, 16], P('dp'), may hold values 0 or 1
- cotangent: bfloat16 [4096, 1024], P(('dp', 'col'), 'row'), may hold values from -6 to 6
Outputs:
- result: bfloat16 [4096, 1024], P(('dp', 'col'), 'row')
- grad_inputs: float32 [4096, 1024], P(('dp', 'col'), 'row')
- grad_norm_in: float32 [1, 1024], P(None, 'row')
- grad_w_proj: float32 [1, 1024, 8, 768], P(None, 'row', 'col')
- grad_w_small: float32 [1, 1024, 8, 2], P(None, 'row', 'col')
- grad_w_conv: float32 [1, 4, 8, 512], P(None, None, 'col')
- grad_a_log: float32 [1, 8], P(None, 'col')
- grad_dt_bias: float32 [1, 8], P(None, 'col')
- grad_norm_out: float32 [1, 256], replicated
- grad_w_out: float32 [1, 8, 256, 1024], P(None, 'col', None, 'row')
- grad_norm_ffn: float32 [1, 1024], P(None, 'row')
- grad_w_gu: float32 [1, 1024, 2, 2816], P(None, 'row', None, 'col')
- grad_w_down: float32 [1, 2816, 1024], P(None, 'col', 'row')
Inputs may be any that keep to these rules, and one draw needn't show every extreme that they name: `block_resets`: 1 marks a block of 64 tokens at which a new segment begins; the first block of every sequence begins one whatever its entry.
All inputs are finite; a program needn't handle non-finite values.
Results may differ from a plain program's by a relative error of at most 0.01505.
Values may be sent and summed in bfloat16 or wider, within the bound.
A program may use at most 128 MiB of HBM per device.

v0:
```python
import jax
import jax.numpy as jnp
from jax import lax
from jax.sharding import PartitionSpec as P

BLOCK = 64


norm_eps = 1e-05
unit_eps = 1e-06
precise = lax.Precision.HIGHEST


def block_flags(block_resets):
    column = lax.broadcasted_iota(jnp.int32, block_resets.shape, 1)
    return jnp.where(column == 0, 1, block_resets).reshape(-1)


def conv_silu(inputs, weights, segment):
    tap_count = weights.shape[0]
    length = inputs.shape[0]
    padded = jnp.concatenate([jnp.zeros((tap_count - 1, inputs.shape[1]), jnp.float32), inputs], 0)
    seg_padded = jnp.concatenate([jnp.full((tap_count - 1,), -1, jnp.int32), segment], 0)
    summed = jnp.zeros_like(inputs)
    for offset in range(tap_count):
        first_row = tap_count - 1 - offset
        shifted = lax.slice_in_dim(padded, first_row, first_row + length, axis=0)
        same_seg = (
            lax.slice_in_dim(seg_padded, first_row, first_row + length, axis=0) == segment
        ).astype(jnp.float32)
        summed = summed + weights[offset] * shifted * same_seg[:, None]
    return jax.nn.silu(summed)


def block_step(carried, pieces):
    queries, keys_now, values, log_decay, beta_rows, reset_now = pieces
    carried = carried * (1.0 - reset_now)
    cumulative = jnp.cumsum(log_decay)
    decays = jnp.exp(cumulative)
    block_size = log_decay.shape[0]
    row_ids = lax.broadcasted_iota(jnp.int32, (block_size, block_size), 0)
    col_ids = lax.broadcasted_iota(jnp.int32, (block_size, block_size), 1)
    lower_incl = row_ids >= col_ids
    lower_strict = row_ids > col_ids
    spread = cumulative[:, None] - cumulative[None, :]
    within = jnp.where(lower_incl, jnp.exp(jnp.where(lower_incl, spread, 0.0)), 0.0)
    key_key = jnp.dot(keys_now, keys_now.T, precision=precise)
    coupling = jnp.where(lower_strict, beta_rows[:, None] * key_key * within, 0.0)
    system = jnp.eye(block_size, dtype=jnp.float32) + coupling
    value_width = values.shape[1]
    targets = jnp.concatenate(
        [beta_rows[:, None] * values, (beta_rows * decays)[:, None] * keys_now], 1
    )
    solved = lax.linalg.triangular_solve(
        system, targets, left_side=True, lower=True, unit_diagonal=True
    )
    updates = solved[:, :value_width] - jnp.dot(solved[:, value_width:], carried, precision=precise)
    scores = jnp.dot(queries, keys_now.T, precision=precise) * within
    output = jnp.dot(queries * decays[:, None], carried, precision=precise) + jnp.dot(
        scores, updates, precision=precise
    )
    remaining = jnp.exp(cumulative[-1] - cumulative)
    new_state = decays[-1] * carried + jnp.dot(
        (keys_now * remaining[:, None]).T, updates, precision=precise
    )
    return (new_state, output)


def delta_rule(queries, keys_all, values, log_decay, beta_rows, reset_flags):
    length = queries.shape[0]
    blocks = length // BLOCK

    def to_blocks(source):
        return source.reshape((blocks, BLOCK) + source.shape[1:])

    initial = jnp.zeros((keys_all.shape[1], values.shape[1]), jnp.float32)
    final_state, outputs = lax.scan(
        jax.checkpoint(block_step),
        initial,
        (
            to_blocks(queries),
            to_blocks(keys_all),
            to_blocks(values),
            to_blocks(log_decay),
            to_blocks(beta_rows),
            reset_flags.astype(jnp.float32),
        ),
    )
    return outputs.reshape(length, values.shape[1])


def mixer_head(projected, small_proj, conv_weights, a_log, dt_bias, gain_out, reset_flags):
    segment = jnp.repeat(jnp.cumsum(reset_flags), BLOCK)
    channels = conv_weights.shape[1]
    value_width = gain_out.shape[0]
    key_width = (channels - value_width) // 2
    mixed_out = conv_silu(projected[:, :channels], conv_weights, segment)
    queries = mixed_out[:, :key_width]
    keys_all = mixed_out[:, key_width : 2 * key_width]
    values = mixed_out[:, 2 * key_width :]
    queries = (
        queries
        * lax.rsqrt(jnp.sum(queries * queries, -1, keepdims=True) + unit_eps)
        * key_width ** (-0.5)
    )
    keys_all = keys_all * lax.rsqrt(jnp.sum(keys_all * keys_all, -1, keepdims=True) + unit_eps)
    beta_rows = jax.nn.sigmoid(small_proj[:, 0])
    log_decay = -jnp.exp(a_log) * jax.nn.softplus(small_proj[:, 1] + dt_bias)
    output = delta_rule(queries, keys_all, values, log_decay, beta_rows, reset_flags)
    gate_rows = projected[:, channels:]
    return (
        output
        * lax.rsqrt(jnp.mean(output * output, -1, keepdims=True) + norm_eps)
        * gain_out
        * jax.nn.silu(gate_rows)
    )


def mixer_heads(projected, small_proj, conv_weights, a_log, dt_bias, gain_out, reset_flags):
    return jax.vmap(mixer_head, in_axes=(1, 1, 1, 0, 0, None, None), out_axes=1)(
        projected, small_proj, conv_weights, a_log, dt_bias, gain_out, reset_flags
    )


def row_total(partial_rows):
    return lax.psum(partial_rows, "row")


def gather_tokens(block_rows):
    return lax.all_gather(block_rows, "col", axis=0, tiled=True)


def scatter_tokens(partial_rows):
    return lax.psum_scatter(partial_rows, "col", scatter_dimension=0, tiled=True)


def norm_forward(residual, gain_row, model_width):
    inverse = lax.rsqrt(row_total(jnp.sum(residual * residual, -1)) / model_width + norm_eps)
    scaled = residual * inverse[:, None]
    return (scaled * gain_row, scaled, inverse)


def norm_backward(grad_normed, scaled, inverse, gain_row, model_width):
    grad_scaled = grad_normed * gain_row
    inner_mean = row_total(jnp.sum(grad_scaled * scaled, -1)) / model_width
    grad_rows = inverse[:, None] * (grad_scaled - scaled * inner_mean[:, None])
    grad_gain = jnp.sum(grad_normed * scaled, 0)
    return (grad_rows, grad_gain)


def reduce_ffn(grad_gu, grad_down):
    return (
        lax.psum(grad_gu.astype(jnp.bfloat16), "dp").astype(jnp.float32),
        lax.psum(grad_down.astype(jnp.bfloat16), "dp").astype(jnp.float32),
    )


def reduce_mixer(grad_proj, grad_small, grad_out):
    return (
        lax.psum(grad_proj.astype(jnp.bfloat16), "dp").astype(jnp.float32),
        lax.psum(grad_small.astype(jnp.bfloat16), "dp").astype(jnp.float32),
        lax.psum(grad_out.astype(jnp.bfloat16), "dp").astype(jnp.float32),
    )


def body(
    inputs,
    norm_in,
    w_proj,
    w_small,
    w_conv,
    a_log,
    dt_bias,
    norm_out,
    w_out,
    norm_ffn,
    w_gu,
    w_down,
    block_resets,
    cotangent,
):
    layer_count = w_proj.shape[0]
    row_width = norm_in.shape[1]
    model_width = row_width * lax.axis_size("row")
    heads_col = w_proj.shape[2]
    heads_dev = heads_col // lax.axis_size("row")
    row_index = lax.axis_index("row")
    col_index = lax.axis_index("col")
    head_first = row_index * heads_dev
    reset_flags = block_flags(block_resets)

    def mixer_closed(projected, small_proj, conv_weights, decay_log, decay_bias, gain_out):
        return mixer_heads(
            projected, small_proj, conv_weights, decay_log, decay_bias, gain_out, reset_flags
        )

    residual = inputs.astype(jnp.float32)
    layer_index = 0
    normed, scaled_in, inverse_in = norm_forward(residual, norm_in[layer_index], model_width)
    gathered_in = gather_tokens(normed.astype(jnp.bfloat16))
    proj_part = jnp.einsum(
        "td,dhp->thp", gathered_in, w_proj[layer_index], preferred_element_type=jnp.float32
    )
    small_part = jnp.einsum(
        "td,dhp->thp", gathered_in, w_small[layer_index], preferred_element_type=jnp.float32
    )
    projected = lax.psum_scatter(proj_part, "row", scatter_dimension=1, tiled=True)
    small_proj = lax.psum_scatter(small_part, "row", scatter_dimension=1, tiled=True)
    local_args = (
        projected,
        small_proj,
        lax.dynamic_slice_in_dim(w_conv[layer_index], head_first, heads_dev, 1),
        lax.dynamic_slice_in_dim(a_log[layer_index], head_first, heads_dev, 0),
        lax.dynamic_slice_in_dim(dt_bias[layer_index], head_first, heads_dev, 0),
        norm_out[layer_index],
    )
    mixed_out, pullback = jax.vjp(
        mixer_closed,
        local_args[0],
        local_args[1],
        local_args[2],
        local_args[3],
        local_args[4],
        local_args[5],
    )
    gathered_heads = lax.all_gather(mixed_out.astype(jnp.bfloat16), "row", axis=1, tiled=True)
    branch = scatter_tokens(
        jnp.einsum(
            "thv,hvd->td", gathered_heads, w_out[layer_index], preferred_element_type=jnp.float32
        )
    )
    middle = residual + branch
    normed_ffn, scaled_ffn, inverse_ffn = norm_forward(middle, norm_ffn[layer_index], model_width)
    gathered_ffn = gather_tokens(normed_ffn.astype(jnp.bfloat16))
    gate_up = lax.psum_scatter(
        jnp.einsum(
            "td,dkf->tkf", gathered_ffn, w_gu[layer_index], preferred_element_type=jnp.float32
        ),
        "row",
        scatter_dimension=0,
        tiled=True,
    )
    hidden = (jax.nn.silu(gate_up[:, 0]) * gate_up[:, 1]).astype(jnp.bfloat16)
    hidden_all = lax.all_gather(hidden, "row", axis=0, tiled=True)
    residual = middle + scatter_tokens(
        jnp.dot(hidden_all, w_down[layer_index], preferred_element_type=jnp.float32)
    )
    kept_values = [
        (
            scaled_in,
            inverse_in,
            gathered_in,
            local_args,
            pullback,
            gathered_heads,
            scaled_ffn,
            inverse_ffn,
            gathered_ffn,
            gate_up,
            hidden_all,
        )
    ]
    result = residual.astype(jnp.bfloat16)
    grad_rows = cotangent.astype(jnp.float32)
    ffn_parts = [None] * layer_count
    mixer_parts = [None] * layer_count
    smalls = [None] * layer_count
    for layer_index in reversed(range(layer_count)):
        (
            scaled_in,
            inverse_in,
            gathered_in,
            local_args,
            pullback,
            gathered_heads,
            scaled_ffn,
            inverse_ffn,
            gathered_ffn,
            gate_up,
            hidden_all,
        ) = kept_values[layer_index]
        grad_branch = gather_tokens(grad_rows.astype(jnp.bfloat16))
        grad_down = jnp.einsum(
            "tf,td->fd", hidden_all, grad_branch, preferred_element_type=jnp.float32
        )
        grad_hidden = lax.psum_scatter(
            jnp.einsum(
                "td,fd->tf", grad_branch, w_down[layer_index], preferred_element_type=jnp.float32
            ),
            "row",
            scatter_dimension=0,
            tiled=True,
        )
        gate_rows = gate_up[:, 0]
        up_rows = gate_up[:, 1]
        sigmoid_gate = jax.nn.sigmoid(gate_rows)
        grad_gate = grad_hidden * up_rows * sigmoid_gate * (1.0 + gate_rows * (1.0 - sigmoid_gate))
        grad_up = grad_hidden * gate_rows * sigmoid_gate
        grad_gate_up = lax.all_gather(
            jnp.stack([grad_gate, grad_up], 1).astype(jnp.bfloat16), "row", axis=0, tiled=True
        )
        grad_gu = jnp.einsum(
            "td,tkf->dkf", gathered_ffn, grad_gate_up, preferred_element_type=jnp.float32
        )
        ffn_parts[layer_index] = (grad_gu, grad_down)
        grad_normed_ffn = scatter_tokens(
            jnp.einsum(
                "tkf,dkf->td", grad_gate_up, w_gu[layer_index], preferred_element_type=jnp.float32
            )
        )
        grad_middle, grad_gain_ffn = norm_backward(
            grad_normed_ffn, scaled_ffn, inverse_ffn, norm_ffn[layer_index], model_width
        )
        grad_middle = grad_rows + grad_middle
        grad_branch = gather_tokens(grad_middle.astype(jnp.bfloat16))
        grad_out = jnp.einsum(
            "thv,td->hvd", gathered_heads, grad_branch, preferred_element_type=jnp.float32
        )
        grad_mixed = lax.psum_scatter(
            jnp.einsum(
                "td,hvd->thv", grad_branch, w_out[layer_index], preferred_element_type=jnp.float32
            ).astype(jnp.bfloat16),
            "row",
            scatter_dimension=1,
            tiled=True,
        ).astype(jnp.float32)
        grad_local = pullback(grad_mixed)
        grad_proj_all, grad_small_all = (
            lax.all_gather(grad_local[0].astype(jnp.bfloat16), "row", axis=1, tiled=True),
            lax.all_gather(grad_local[1].astype(jnp.bfloat16), "row", axis=1, tiled=True),
        )
        grad_proj = jnp.einsum(
            "td,thp->dhp", gathered_in, grad_proj_all, preferred_element_type=jnp.float32
        )
        grad_small = jnp.einsum(
            "td,thp->dhp", gathered_in, grad_small_all, preferred_element_type=jnp.float32
        )
        grad_normed_in = scatter_tokens(
            jnp.einsum(
                "thp,dhp->td",
                grad_proj_all,
                w_proj[layer_index],
                preferred_element_type=jnp.float32,
            )
            + jnp.einsum(
                "thp,dhp->td",
                grad_small_all,
                w_small[layer_index],
                preferred_element_type=jnp.float32,
            )
        )
        grad_in, grad_gain_in = norm_backward(
            grad_normed_in, scaled_in, inverse_in, norm_in[layer_index], model_width
        )
        grad_rows = grad_middle + grad_in
        mixer_parts[layer_index] = reduce_mixer(grad_proj, grad_small, grad_out)
        smalls[layer_index] = (
            grad_gain_in,
            grad_gain_ffn,
            grad_local[2],
            grad_local[3],
            grad_local[4],
            grad_local[5],
        )
    ffn_parts = [reduce_ffn(layer_grads[0], layer_grads[1]) for layer_grads in ffn_parts]
    stacked_gu = jnp.stack([layer_grads[0] for layer_grads in ffn_parts], 0)
    stacked_down = jnp.stack([layer_grads[1] for layer_grads in ffn_parts], 0)
    stacked_proj = jnp.stack([layer_grads[0] for layer_grads in mixer_parts], 0)
    stacked_small = jnp.stack([layer_grads[1] for layer_grads in mixer_parts], 0)
    stacked_out = jnp.stack([layer_grads[2] for layer_grads in mixer_parts], 0)
    head_global = col_index * heads_col + head_first
    total_heads = heads_col * lax.axis_size("col")
    gain_in_full = lax.dynamic_update_slice_in_dim(
        jnp.zeros((layer_count, model_width), jnp.float32),
        jnp.stack([layer_small[0] for layer_small in smalls], 0),
        row_index * row_width,
        1,
    )
    gain_ffn_full = lax.dynamic_update_slice_in_dim(
        jnp.zeros((layer_count, model_width), jnp.float32),
        jnp.stack([layer_small[1] for layer_small in smalls], 0),
        row_index * row_width,
        1,
    )
    conv_full = lax.dynamic_update_slice_in_dim(
        jnp.zeros((layer_count, w_conv.shape[1], total_heads, w_conv.shape[3]), jnp.float32),
        jnp.stack([layer_small[2] for layer_small in smalls], 0),
        head_global,
        2,
    )
    alog_full = lax.dynamic_update_slice_in_dim(
        jnp.zeros((layer_count, total_heads), jnp.float32),
        jnp.stack([layer_small[3] for layer_small in smalls], 0),
        head_global,
        1,
    )
    bias_full = lax.dynamic_update_slice_in_dim(
        jnp.zeros((layer_count, total_heads), jnp.float32),
        jnp.stack([layer_small[4] for layer_small in smalls], 0),
        head_global,
        1,
    )
    gain_out_sum = jnp.stack([layer_small[5] for layer_small in smalls], 0)
    summed = lax.psum(
        (gain_in_full, gain_ffn_full, conv_full, alog_full, bias_full, gain_out_sum),
        ("dp", "row", "col"),
    )
    col_first = col_index * heads_col
    grad_norm_in = lax.dynamic_slice_in_dim(summed[0], row_index * row_width, row_width, 1)
    grad_norm_ffn = lax.dynamic_slice_in_dim(summed[1], row_index * row_width, row_width, 1)
    grad_conv = lax.dynamic_slice_in_dim(summed[2], col_first, heads_col, 2)
    grad_alog = lax.dynamic_slice_in_dim(summed[3], col_first, heads_col, 1)
    grad_bias = lax.dynamic_slice_in_dim(summed[4], col_first, heads_col, 1)
    return (
        result,
        grad_rows,
        grad_norm_in,
        stacked_proj,
        stacked_small,
        grad_conv,
        grad_alog,
        grad_bias,
        summed[5],
        stacked_out,
        grad_norm_ffn,
        stacked_gu,
        stacked_down,
    )


def solution(mesh):
    in_specs = (
        P(("dp", "col"), "row"),
        P(None, "row"),
        P(None, "row", "col", None),
        P(None, "row", "col", None),
        P(None, None, "col", None),
        P(None, "col"),
        P(None, "col"),
        P(),
        P(None, "col", None, "row"),
        P(None, "row"),
        P(None, "row", None, "col"),
        P(None, "col", "row"),
        P("dp", None),
        P(("dp", "col"), "row"),
    )
    out_specs = (
        P(("dp", "col"), "row"),
        P(("dp", "col"), "row"),
        P(None, "row"),
        P(None, "row", "col", None),
        P(None, "row", "col", None),
        P(None, None, "col", None),
        P(None, "col"),
        P(None, "col"),
        P(),
        P(None, "col", None, "row"),
        P(None, "row"),
        P(None, "row", None, "col"),
        P(None, "col", "row"),
    )
    return jax.shard_map(body, mesh=mesh, in_specs=in_specs, out_specs=out_specs, check_vma=False)
```

profile of v0, /device:TPU:0, one launch (start us, length us, event | category | flops | bytes accessed | tf_op | source)
XLA Modules:
  0.0 1444.2 jit_solution(17535072759686358500)
XLA Ops:
  12.9 30.6 %all-gather.9.cloned.1.call-done = bf16[1024,512]{1,0:T(8,128)(2,1)} async-done(((bf16[256,512]{1,0:T(8,128)(2,1)}), bf16[1024,512]{1,0:T(8,128)(2,1)}) %all-gather.9.cloned.1.call-update) | async-done | bytes 1048592 | tf_op jit(solution)/shard_map/all_gather | solution.py:130
  43.5 5.7 fusion.168
  71.1 260.4 %while.44 = (s32[]{:T(128)}, f32[1,128,256]{2,1,0:T(8,128)S(1)}, f32[16,1,64,256]{3,2,1,0:T(8,128)S(1)}, f32[16,1,128,256]{3,2,1,0:T(8,128)}, f32[16,1,64]{2,1,0...) while((s32[]{:T(128)}, f32[1,128,256]{2,1,0:T(8,128)S(1)}, ...), condition=%wide.region_9.11_spmd.clone.clone, body=%wide.region_7.10_spmd.clone.clone.sunk | while | flops 120021120 | bytes 1927154 | solution.py:77
  78.4 4.9 custom-call.26
  94.7 4.9 custom-call.26
  143.5 4.9 custom-call.26
  192.3 4.9 custom-call.26
  241.2 4.9 custom-call.26
  257.4 4.9 custom-call.26
  273.7 4.9 custom-call.26
  290.0 4.9 custom-call.26
  306.3 4.9 custom-call.26
  322.6 4.9 custom-call.26
  335.9 10.3 all-gather.11.cloned.1.call-done
  350.1 44.5 %reduce-scatter.11.cloned.1.call-done = f32[256,512]{1,0:T(8,128)} async-done(((f32[1024,512]{1,0:T(8,128)}), f32[256,512]{1,0:T(8,128)}) %reduce-scatter.11.cloned.1.call-update) | async-done | bytes 524304 | tf_op jit(solution)/shard_map/reduce_scatter | solution.py:134
  399.2 24.1 %all-gather.17.cloned.1.call-done = bf16[1024,512]{1,0:T(8,128)(2,1)} async-done(((bf16[256,512]{1,0:T(8,128)(2,1)}), bf16[1024,512]{1,0:T(8,128)(2,1)}) %all-gather.17.cloned.1.call-update) | async-done | bytes 1048592 | tf_op jit(solution)/shard_map/all_gather | solution.py:130
  427.4 25.4 %all-gather.13.cloned.1.call-done = bf16[1024,512]{1,0:T(8,128)(2,1)} async-done(((bf16[256,512]{1,0:T(8,128)(2,1)}), bf16[1024,512]{1,0:T(8,128)(2,1)}) %all-gather.13.cloned.1.call-update) | async-done | bytes 1048592 | tf_op jit(solution)/shard_map/all_gather | solution.py:130
  452.8 5.9 fusion.164
  458.8 6.9 reduce-scatter.17.cloned.1.call-done
  465.6 17.5 %reduce-scatter.13.cloned.1.call-done = f32[512,2,704]{0,2,1:T(8,128)} async-done(((f32[1024,2,704]{0,2,1:T(8,128)}), f32[512,2,704]{0,2,1:T(8,128)}) %reduce-scatter.13.cloned.1.call-update) | async-done | bytes 2883600 | tf_op jit(solution)/shard_map/reduce_scatter | solution.py:235
  488.6 12.9 all-gather.19.cloned.1.call-done
  501.6 5.4 convolution_bitcast_fusion.13
  507.0 45.1 %reduce-scatter.19.cloned.1.call-done = f32[256,512]{1,0:T(8,128)} async-done(((f32[1024,512]{1,0:T(8,128)}), f32[256,512]{1,0:T(8,128)}) %reduce-scatter.19.cloned.1.call-update) | async-done | bytes 524304 | tf_op jit(solution)/shard_map/reduce_scatter | solution.py:134
  558.5 27.4 %all-gather.21.cloned.1.call-done = bf16[1024,512]{1,0:T(8,128)(2,1)} async-done(((bf16[256,512]{1,0:T(8,128)(2,1)}), bf16[1024,512]{1,0:T(8,128)(2,1)}) %all-gather.21.cloned.1.call-update) | async-done | bytes 1048592 | tf_op jit(solution)/shard_map/all_gather | solution.py:130
  589.0 8.1 reduce-scatter.21.cloned.1.call-done
  605.1 456.7 %while.43 = (s32[]{:T(128)}, f32[1,128,256]{1,2,0:T(8,128)S(1)}, f32[16,1,64,128]{3,2,1,0:T(8,128)}, f32[16,1,64,128]{3,2,1,0:T(8,128)}, f32[16,1,64,256]{3,2,1,...) while((s32[]{:T(128)}, f32[1,128,256]{1,2,0:T(8,128)S(1)}, ...), condition=%wide.region_34.36_spmd.clone, body=%wide.region_22.35_spmd.clone.sunk | while | flops 299885248 | bytes 5738839 | solution.py:77
  617.9 4.9 custom-call.25
  641.1 4.9 custom-call.24
  675.0 4.9 custom-call.25
  698.2 4.9 custom-call.24
  726.7 4.9 custom-call.24
  760.6 4.9 custom-call.25
  783.8 4.9 custom-call.24
  817.7 4.9 custom-call.25
  840.9 4.9 custom-call.24
  874.8 4.9 custom-call.25
  903.4 4.9 custom-call.25
  931.9 4.9 custom-call.25
  960.5 4.9 custom-call.25
  983.6 4.9 custom-call.24
  1017.5 4.9 custom-call.25
  1080.1 7.2 all-gather.23.cloned.1.call-done
  1092.9 6.6 all-gather.15.cloned.1.call-done
  1118.5 10.1 psum.111
  1130.0 94.2 %all-reduce.27.cloned.1.call-done = f32[1,4,8,512]{3,2,1,0:T(8,128)} async-done(((f32[1,4,8,512]{3,2,1,0:T(8,128)}), f32[1,4,8,512]{3,2,1,0:T(8,128)}) %all-reduce.27.cloned.1.call-update) | async-done | bytes 65552 | tf_op jit(solution)/shard_map/psum | solution.py:404
  1225.7 46.0 %reduce-scatter.23.cloned.1.call-done = f32[256,512]{1,0:T(8,128)} async-done(((f32[1024,512]{1,0:T(8,128)}), f32[256,512]{1,0:T(8,128)}) %reduce-scatter.23.cloned.1.call-update) | async-done | bytes 524304 | tf_op jit(solution)/shard_map/reduce_scatter | solution.py:134
  1275.4 43.7 %all-reduce.22 = (f32[1,1024]{1,0:T(1,128)S(1)}, f32[1,8]{1,0:T(1,128)S(1)}, f32[1,8]{1,0:T(1,128)S(1)}, f32[1,256]{1,0:T(1,128)}, f32[1,1024]{1,0:T(1,128)S(1)}) all-reduce(f32[1,1024]{1,0:T(1,128)S(1)} %constant_dynamic-update-slice_fusion.3, ...), channel_id=1, replica_groups=mesh['dp'=4,'row'=2,'col'=4] {'dp','row','col'}, use_global_device_ids=true, to_apply=%region_41.43 | all-reduce | flops 2320 | bytes 18560 | tf_op jit(solution)/shard_map/psum | solution.py:404
  1323.8 104.3 %all-reduce.29.cloned.1.call-done = (bf16[1,512,2,768]{3,1,2,0:T(8,128)(2,1)}, bf16[1,2,256,512]{3,2,1,0:T(8,128)(2,1)}, bf16[1,512,2,704]{1,3,2,0:T(8,128)(2,1)}, bf16[1,704,512]{2,1,0:T(8,128)(2,1)}) async-done(((bf16[1,512,2,768]{3,1,2,0:T(8,128)(2,1)}, bf16[1,2,256,512]{3,2,1,0:T(8,128)(2,1)}, bf16[1,512,2,704]{1,3,2,0:T(8,128)(2,1)}, bf16[1,704,512]{2,1,0:T(8,128)(2,1)}), ...) | async-done | bytes 4259856 | tf_op jit(solution)/shard_map/psum | solution.py:160
  (1307 shorter events, 699.1 us)
Async XLA Ops:
  7.2 36.3 %copy-start = (bf16[1,512,2,768]{3,2,1,0:T(2,128)(2,1)S(1)}, bf16[1,512,2,768]{3,2,1,0:T(2,128)(2,1)}, u32[]{:S(2)}) copy-start(bf16[1,512,2,768]{3,2,1,0:T(2,128)(2,1)} %param.22) | copy-start | bytes 4718596
  7.2 36.3 %all-gather.9.cloned.1.call-start = ((), (), s32[]{:S(2)}) async-start(), calls=%async_computation.8 | async-start | bytes 1310720 | tf_op jit(solution)/shard_map/all_gather | solution.py:130
  11.0 38.2 %copy-start.55 = (f32[256]{0:T(256)}, f32[256]{0:T(256)S(1)}, u32[]{:S(2)}) copy-start(f32[256]{0:T(256)S(1)} %add_rsqrt_fusion.3) | copy-start | bytes 3076
  12.8 50.6 %reduce-scatter.9.cloned.1.call-start = ((), (), s32[]{:S(2)}) async-start(), calls=%async_computation.9 | async-start | bytes 9437184 | tf_op jit(solution)/shard_map/reduce_scatter | solution.py:207
  49.3 296.9 %all-gather.11.cloned.1.call-start = ((), (), s32[]{:S(2)}) async-start(), calls=%async_computation.10 | async-start | bytes 1572864 | tf_op jit(solution)/shard_map/all_gather | solution.py:226
  52.7 12.5 copy-start.42
  52.8 12.5 copy-start.44
  52.8 12.5 copy-start.46
  52.8 12.5 copy-start.48
  52.9 12.4 copy-start.22
  52.9 12.4 copy-start.24
  52.9 12.4 copy-start.26
  56.6 8.6 copy-start.28
  59.6 5.6 copy-start.20
  71.1 262.3 %copy-start.51 = (f32[1,256]{1,0:T(1,128)S(1)}, f32[1,256]{1,0:T(1,128)}, u32[]{:S(2)}) copy-start(f32[1,256]{1,0:T(1,128)} %param.27) | copy-start | bytes 3076
  332.8 13.4 copy-start.17
  333.4 16.0 %copy-start.35 = (f32[1024]{0:T(1024)}, f32[1024]{0:T(1024)S(1)}, u32[]{:S(2)}) copy-start(f32[1024]{0:T(1024)S(1)} %rsqrt.48) | copy-start | bytes 12292
  335.8 58.8 %reduce-scatter.11.cloned.1.call-start = ((), (), s32[]{:S(2)}) async-start(), calls=%async_computation.11 | async-start | bytes 2621440 | tf_op jit(solution)/shard_map/reduce_scatter | solution.py:134
  349.5 45.2 %copy-start.5 = (bf16[256,512]{1,0:T(8,128)(2,1)S(1)}, bf16[256,512]{1,0:T(8,128)(2,1)}, u32[]{:S(2)}) copy-start(bf16[256,512]{1,0:T(8,128)(2,1)} %param.20) | copy-start | bytes 786436
  349.5 48.9 %copy-start.37 = (f32[1,512]{1,0:T(1,128)S(1)}, f32[1,512]{1,0:T(1,128)}, u32[]{:S(2)}) copy-start(f32[1,512]{1,0:T(1,128)} %param.29) | copy-start | bytes 6148
  349.5 73.9 %all-gather.17.cloned.1.call-start = ((), (), s32[]{:S(2)}) async-start(), calls=%async_computation.16 | async-start | bytes 1310720 | tf_op jit(solution)/shard_map/all_gather | solution.py:130
  350.1 102.7 %all-gather.13.cloned.1.call-start = ((), (), s32[]{:S(2)}) async-start(), calls=%async_computation.12 | async-start | bytes 1310720 | tf_op jit(solution)/shard_map/all_gather | solution.py:130
  398.3 158.1 %copy-start.39 = (f32[256]{0:T(256)}, f32[256]{0:T(256)S(1)}, u32[]{:S(2)}) copy-start(f32[256]{0:T(256)S(1)} %add_rsqrt_fusion.2) | copy-start | bytes 3076
  399.2 66.4 %reduce-scatter.17.cloned.1.call-start = ((), (), s32[]{:S(2)}) async-start(), calls=%async_computation.17 | async-start | bytes 4325376 | tf_op jit(solution)/shard_map/reduce_scatter | solution.py:286
  427.3 55.8 %reduce-scatter.13.cloned.1.call-start = ((), (), s32[]{:S(2)}) async-start(), calls=%async_computation.13 | async-start | bytes 8650752 | tf_op jit(solution)/shard_map/reduce_scatter | solution.py:235
  458.7 42.8 %all-gather.19.cloned.1.call-start = ((), (), s32[]{:S(2)}) async-start(), calls=%async_computation.18 | async-start | bytes 4325376 | tf_op jit(solution)/shard_map/all_gather | solution.py:299
  488.4 63.7 %reduce-scatter.19.cloned.1.call-start = ((), (), s32[]{:S(2)}) async-start(), calls=%async_computation.19 | async-start | bytes 2621440 | tf_op jit(solution)/shard_map/reduce_scatter | solution.py:134
  506.9 78.9 %all-gather.21.cloned.1.call-start = ((), (), s32[]{:S(2)}) async-start(), calls=%async_computation.20 | async-start | bytes 1310720 | tf_op jit(solution)/shard_map/all_gather | solution.py:130
  556.4 32.5 %copy-start.59 = (f32[256]{0:T(256)}, f32[256]{0:T(256)S(1)}, u32[]{:S(2)}) copy-start(f32[256]{0:T(256)S(1)} %broadcast_multiply_fusion.6) | copy-start | bytes 3076
  558.5 38.7 %reduce-scatter.21.cloned.1.call-start = ((), (), s32[]{:S(2)}) async-start(), calls=%async_computation.21 | async-start | bytes 1572864 | tf_op jit(solution)/shard_map/reduce_scatter | solution.py:319
  589.0 498.3 %all-gather.23.cloned.1.call-start = ((), (), s32[]{:S(2)}) async-start(), calls=%async_computation.22 | async-start | bytes 4718592 | tf_op jit(solution)/shard_map/all_gather | solution.py:329
  1073.8 25.6 %all-gather.15.cloned.1.call-start = ((), (), s32[]{:S(2)}) async-start(), calls=%async_computation.14 | async-start | bytes 2162688 | tf_op jit(solution)/shard_map/all_gather | solution.py:244
  1074.4 149.8 %all-reduce.27.cloned.1.call-start = ((), (), s32[]{:S(2)}) async-start(), calls=%async_computation.24 | async-start | bytes 131072 | tf_op jit(solution)/shard_map/psum | solution.py:404
  1079.8 11.2 copy-start.54
  1079.9 191.8 %reduce-scatter.23.cloned.1.call-start = ((), (), s32[]{:S(2)}) async-start(), calls=%async_computation.23 | async-start | bytes 2621440 | tf_op jit(solution)/shard_map/reduce_scatter | solution.py:134
  1092.8 6.7 copy-start.15
  1092.8 228.6 %reduce-scatter.15.cloned.1.call-start = ((), (), s32[]{:S(2)}) async-start(), calls=%async_computation.15 | async-start | bytes 2621440 | tf_op jit(solution)/shard_map/reduce_scatter | solution.py:134
  1103.2 324.9 %all-reduce.29.cloned.1.call-start = ((), (), s32[]{:S(2)}) async-start(), calls=%async_computation.25 | async-start | bytes 8519680 | tf_op jit(solution)/shard_map/psum | solution.py:160
  1115.1 156.5 %copy-start.50 = (f32[1,512]{1,0:T(1,128)S(1)}, f32[1,512]{1,0:T(1,128)}, u32[]{:S(2)}) copy-start(f32[1,512]{1,0:T(1,128)} %param.21) | copy-start | bytes 6148
  1115.1 156.5 %copy-start.56 = (f32[256]{0:T(256)S(1)}, f32[256]{0:T(256)}, u32[]{:S(2)}) copy-start(f32[256]{0:T(256)} %copy-done.55) | copy-start | bytes 3076
  1115.1 160.3 %copy-start.62 = (f32[256]{0:T(256)S(1)}, f32[256]{0:T(256)}, u32[]{:S(2)}) copy-start(f32[256]{0:T(256)} %get-tuple-element.731) | copy-start | bytes 3076
  1115.1 206.3 %copy-start.6 = (f32[256,512]{1,0:T(8,128)S(1)}, f32[256,512]{1,0:T(8,128)}, u32[]{:S(2)}) copy-start(f32[256,512]{1,0:T(8,128)} %reduce-scatter.19.cloned.1.call-done) | copy-start | bytes 1572868
  1115.1 206.3 %copy-start.12 = (bf16[256,512]{1,0:T(8,128)(2,1)S(1)}, bf16[256,512]{1,0:T(8,128)(2,1)}, u32[]{:S(2)}) copy-start(bf16[256,512]{1,0:T(8,128)(2,1)} %param.33) | copy-start | bytes 786436
  1115.1 206.3 %copy-start.38 = (f32[1,512]{1,0:T(1,128)S(1)}, f32[1,512]{1,0:T(1,128)}, u32[]{:S(2)}) copy-start(f32[1,512]{1,0:T(1,128)} %param.29) | copy-start | bytes 6148
  1115.1 206.3 %copy-start.40 = (f32[256]{0:T(256)S(1)}, f32[256]{0:T(256)}, u32[]{:S(2)}) copy-start(f32[256]{0:T(256)} %copy-done.39) | copy-start | bytes 3076
  1115.1 206.3 %copy-start.60 = (f32[256]{0:T(256)S(1)}, f32[256]{0:T(256)}, u32[]{:S(2)}) copy-start(f32[256]{0:T(256)} %copy-done.59) | copy-start | bytes 3076
  1428.1 4.8 copy-start.18
  1428.2 5.9 copy-start.13
  (44 other events, 106.1 us)
Sparse Core Ops, SparseCore 0:
  13.0 30.5 all-gather.8
  49.4 14.0 reduce-scatter.8
  335.9 10.2 all-gather.10
  349.6 45.0 reduce-scatter.10
  396.1 27.2 all-gather.16
  425.4 27.4 all-gather.12
  455.6 9.9 reduce-scatter.16
  468.0 15.0 reduce-scatter.12
  488.5 12.9 all-gather.18
  507.1 45.0 reduce-scatter.18
  558.6 27.2 all-gather.20
  589.1 8.0 reduce-scatter.20
  1074.0 13.2 all-gather.22
  1088.7 10.7 all-gather.14
  1105.5 118.6 all-reduce.26
  1226.9 44.6 reduce-scatter.22
  1274.4 44.1 reduce-scatter.14
  1322.9 105.2 all-reduce.28
where the time goes:
time: 1460 us; the launch traced here: 1440 us
  waiting for transfers between devices  516 us (35%)
  other arithmetic  434 us (30%)
  matrix products  252 us (17%)
  local copies, waits for them, and re-layouts  132 us (9%)
  blocking collectives  68.9 us (5%)
  loops' own time  23.7 us (2%)
  between operations  17.1 us (1%)
    another operation x112, other arithmetic, block_step(): lax.linalg.triangular_solve(system, targets, left_side=True, lower=True,...  238 us
    reduce_scatter x4, waiting for transfers between devices, scatter_tokens(): lax.psum_scatter(partial_rows, 'col', scatter_dimension=0, tiled=True)  136 us
    all_gather x4, waiting for transfers between devices, gather_tokens(): return lax.all_gather(block_rows, 'col', axis=0, tiled=True)  108 us
    psum x1, waiting for transfers between devices, reduce_mixer(): lax.psum(grad_proj.astype(jnp.bfloat16), 'dp').astype(jnp.float32)  104 us
    psum x1, waiting for transfers between devices, body(): lax.psum((gain_in_full, gain_ffn_full, conv_full, alog_full, bias_full, g...  94.2 us
    dot_general x64, matrix products, block_step(): scores = jnp.dot(queries, keys_now.T, precision=precise) * within  47.1 us
    another operation x64, other arithmetic, block_step(): cumulative = jnp.cumsum(log_decay)  45.9 us
    psum x1, blocking collectives, body(): lax.psum((gain_in_full, gain_ffn_full, conv_full, alog_full, bias_full, g...  43.7 us
  transfers between devices with their start and end apart: 18, of which 17 were waited for; matrix products, arithmetic and copies ran while one was open for 4% of the time, Pallas kernels for 0%

commit v1 on v0

v1 whole, which is shorter than its diff:
```python
import jax
import jax.numpy as jnp
from jax import lax
from jax.experimental import pallas as pl
from jax.experimental.pallas import tpu as pltpu
from jax.sharding import PartitionSpec as P

BLOCK = 64
norm_eps = 1e-05
unit_eps = 1e-06


def block_flags(block_resets):
    column = lax.broadcasted_iota(jnp.int32, block_resets.shape, 1)
    return jnp.where(column == 0, 1, block_resets).reshape(-1)


SUPER = 256


def contract(left, right, left_dim, right_dim):
    dims = (((left_dim,), (right_dim,)), ((), ()))
    left_hi = left.astype(jnp.bfloat16)
    right_hi = right.astype(jnp.bfloat16)
    left_lo = (left - left_hi.astype(jnp.float32)).astype(jnp.bfloat16)
    right_lo = (right - right_hi.astype(jnp.float32)).astype(jnp.bfloat16)

    def single(one, other):
        return lax.dot_general(one, other, dims, preferred_element_type=jnp.float32)

    return single(left_hi, right_hi) + (single(left_hi, right_lo) + single(left_lo, right_hi))


@jax.custom_vjp
def nn(left, right):
    return contract(left, right, 1, 0)


@jax.custom_vjp
def nt(left, right):
    return contract(left, right, 1, 1)


@jax.custom_vjp
def tn(left, right):
    return contract(left, right, 0, 0)


nn.defvjp(lambda a, b: (nn(a, b), (a, b)), lambda k, g: (nt(g, k[1]), tn(k[0], g)))
nt.defvjp(lambda a, b: (nt(a, b), (a, b)), lambda k, g: (nn(g, k[1]), tn(g, k[0])))
tn.defvjp(lambda a, b: (tn(a, b), (a, b)), lambda k, g: (nt(k[1], g), nn(k[0], g)))


@jax.custom_vjp
def solve(inverse, coupling, targets):
    return nn(inverse, targets)


def solve_fwd(inverse, coupling, targets):
    solved = nn(inverse, targets)
    return solved, (inverse, solved)


def solve_bwd(kept, grad):
    inverse, solved = kept
    grad_targets = tn(inverse, grad)
    return jnp.zeros_like(inverse), -nt(grad_targets, solved), grad_targets


solve.defvjp(solve_fwd, solve_bwd)


def block_masks():
    rows = lax.broadcasted_iota(jnp.int32, (SUPER, SUPER), 0)
    cols = lax.broadcasted_iota(jnp.int32, (SUPER, SUPER), 1)
    shift = BLOCK.bit_length() - 1
    same = (rows >> shift) == (cols >> shift)
    return rows, cols, same


def unit_lower_inverse(coupling, rows, cols):
    eye = jnp.where(rows == cols, 1.0, 0.0)
    inverse = None
    for level in range(BLOCK.bit_length() - 1):
        pair = ((rows >> (level + 1)) == (cols >> (level + 1))) & (
            ((rows >> level) & 1) > ((cols >> level) & 1)
        )
        corner = jnp.where(pair, coupling, 0.0)
        if inverse is None:
            inverse = eye - corner
        else:
            inverse = inverse - nn(nn(inverse, corner), inverse)
    return inverse


def intra(query_act, key_act, values, beta, log_decay, inverse, masks):
    rows, cols, same = masks
    key_width = query_act.shape[1]
    queries = (
        query_act
        * lax.rsqrt(jnp.sum(query_act * query_act, -1, keepdims=True) + unit_eps)
        * key_width ** (-0.5)
    )
    keys_all = key_act * lax.rsqrt(jnp.sum(key_act * key_act, -1, keepdims=True) + unit_eps)
    eye = jnp.where(rows == cols, 1.0, 0.0)
    upto = jnp.where(same & (rows <= cols), 1.0, 0.0)
    sames = jnp.where(same, 1.0, 0.0)
    lower = same & (rows >= cols)
    strict = same & (rows > cols)
    cum_row = jnp.sum(log_decay * upto, 0, keepdims=True)
    total_row = jnp.sum(log_decay * sames, 0, keepdims=True)
    cum = jnp.sum(cum_row * eye, 1, keepdims=True)
    total = jnp.sum(total_row * eye, 1, keepdims=True)
    decays = jnp.exp(cum)
    within = jnp.where(lower, jnp.exp(jnp.where(lower, cum - cum_row, 0.0)), 0.0)
    coupling = jnp.where(strict, beta * nt(keys_all, keys_all) * within, 0.0)
    if inverse is None:
        inverse = unit_lower_inverse(coupling, rows, cols)
    solved_v = solve(inverse, coupling, beta * values)
    solved_k = solve(inverse, coupling, (beta * decays) * keys_all)
    scores = nt(queries, keys_all) * within
    return (
        solved_v,
        solved_k,
        scores,
        queries * decays,
        keys_all * jnp.exp(total - cum),
        jnp.exp(total),
    ), inverse


def gated(output, gate, gain):
    scaled = output * lax.rsqrt(jnp.mean(output * output, -1, keepdims=True) + norm_eps)
    return scaled * gain * (gate * lax.logistic(gate))


def gates(small, a_log, dt_bias):
    beta = lax.logistic(small[:, 0:1])
    shifted = small[:, 1:2] + dt_bias
    soft = jnp.maximum(shifted, 0.0) + jnp.log1p(jnp.exp(-jnp.abs(shifted)))
    return beta, -jnp.exp(a_log) * soft, shifted


def fill_padded(padded, projected_ref, channels):
    padded[0:8, :] = jnp.zeros((8, channels), jnp.float32)
    padded[8:, :] = projected_ref[:, :channels]


def taps_kept(reset_rows, offset):
    place = lax.broadcasted_iota(jnp.int32, reset_rows.shape, 0) & (BLOCK - 1)
    return jnp.where(place < offset, 1.0 - reset_rows, 1.0)


def convolve(padded, conv_ref, reset_rows, first):
    summed = None
    for offset in range(conv_ref.shape[0]):
        term = conv_ref[offset : offset + 1, :] * padded[pl.ds(8 + first - offset, SUPER), :]
        if offset:
            term = term * taps_kept(reset_rows, offset)
        summed = term if summed is None else summed + term
    return summed


def forward_kernel(
    projected_ref, small_ref, reset_ref, conv_ref, alog_ref, bias_ref, gain_ref,
    mixed_ref, output_ref, inverse_ref, state_ref, update_ref, padded,
):
    length = projected_ref.shape[0]
    channels = conv_ref.shape[1]
    value_width = gain_ref.shape[1]
    key_width = (channels - value_width) // 2
    masks = block_masks()
    fill_padded(padded, projected_ref, channels)
    pieces = []
    for first in range(0, length, SUPER):
        span = slice(first, first + SUPER)
        summed = convolve(padded, conv_ref, reset_ref[span, :], first)
        act = summed * lax.logistic(summed)
        beta, log_decay, _ = gates(small_ref[span, :], alog_ref[...], bias_ref[...])
        made, inverse = intra(
            act[:, :key_width], act[:, key_width : 2 * key_width], act[:, 2 * key_width :],
            beta, log_decay, None, masks,
        )
        inverse_ref[span, :] = inverse
        pieces.append(made)
    state = jnp.zeros((key_width, value_width), jnp.float32)
    for index, first in enumerate(range(0, length, SUPER)):
        solved_v, solved_k, scores, query_decay, key_rest, last = pieces[index]
        updates, reads = [], []
        for start in range(0, SUPER, BLOCK):
            part = slice(start, start + BLOCK)
            block = (first + start) // BLOCK
            reset_now = reset_ref[first + start : first + start + 1, :]
            state = state * (1.0 - reset_now)
            state_ref[block * key_width : (block + 1) * key_width, :] = state
            transfer = tn(key_rest[part], solved_k[part])
            added = tn(key_rest[part], solved_v[part])
            updates.append(solved_v[part] - nn(solved_k[part], state))
            reads.append(nn(query_decay[part], state))
            state = last[start : start + 1, :] * state + added - nn(transfer, state)
        update = jnp.concatenate(updates, 0)
        output = jnp.concatenate(reads, 0) + nn(scores, update)
        span = slice(first, first + SUPER)
        update_ref[span, :] = update
        output_ref[span, :] = output
        mixed_ref[span, :] = gated(output, projected_ref[span, channels:], gain_ref[...]).astype(
            mixed_ref.dtype
        )


def backward_kernel(
    projected_ref, small_ref, reset_ref, conv_ref, alog_ref, bias_ref, gain_ref,
    output_ref, inverse_ref, state_ref, update_ref, grad_ref,
    dproj_ref, dsmall_ref, dconv_ref, dalog_ref, dbias_ref, dgain_ref, padded, dpadded,
):
    length = projected_ref.shape[0]
    channels = conv_ref.shape[1]
    value_width = gain_ref.shape[1]
    key_width = (channels - value_width) // 2
    tap_count = conv_ref.shape[0]
    masks = block_masks()
    fill_padded(padded, projected_ref, channels)
    dpadded[length:, :] = jnp.zeros((8, channels), jnp.float32)
    dstate = jnp.zeros((key_width, value_width), jnp.float32)
    dgain = jnp.zeros((1, value_width), jnp.float32)
    dalog = jnp.zeros((1, 1), jnp.float32)
    dbias = jnp.zeros((1, 1), jnp.float32)
    dconv = [jnp.zeros((1, channels), jnp.float32) for _ in range(tap_count)]
    for first in reversed(range(0, length, SUPER)):
        span = slice(first, first + SUPER)
        _, pull_gated = jax.vjp(
            gated, output_ref[span, :], projected_ref[span, channels:], gain_ref[...]
        )
        doutput, dgate, dgain_part = pull_gated(grad_ref[span, :].astype(jnp.float32))
        dgain = dgain + dgain_part
        dproj_ref[span, channels:] = dgate.astype(dproj_ref.dtype)
        summed = convolve(padded, conv_ref, reset_ref[span, :], first)
        gate_of = lax.logistic(summed)
        act = summed * gate_of
        beta, log_decay, shifted = gates(small_ref[span, :], alog_ref[...], bias_ref[...])
        inverse = inverse_ref[span, :]
        made, pull_intra = jax.vjp(
            lambda q, k, v, b, g: intra(q, k, v, b, g, inverse, masks)[0],
            act[:, :key_width], act[:, key_width : 2 * key_width], act[:, 2 * key_width :],
            beta, log_decay,
        )
        _, solved_k, scores, query_decay, key_rest, last = made
        update = update_ref[span, :]
        dscores = nt(doutput, update)
        through = tn(scores, doutput)
        dupdates, dsolved_k, dquery, dkey, dlast = [], [], [], [], []
        for start in reversed(range(0, SUPER, BLOCK)):
            part = slice(start, start + BLOCK)
            block = (first + start) // BLOCK
            reset_now = reset_ref[first + start : first + start + 1, :]
            state = state_ref[block * key_width : (block + 1) * key_width, :]
            last_now = last[start : start + 1, :]
            transfer = tn(solved_k[part], key_rest[part])
            given = tn(query_decay[part], doutput[part]) - tn(solved_k[part], through[part])
            dupdate = through[part] + nn(key_rest[part], dstate)
            dupdates.append(dupdate)
            dsolved_k.append(-nt(dupdate, state))
            dquery.append(nt(doutput[part], state))
            dkey.append(nt(update[part], dstate))
            inner = jnp.sum(
                jnp.sum(state * dstate, 1, keepdims=True), 0, keepdims=True
            )
            place = lax.broadcasted_iota(jnp.int32, (BLOCK, 1), 0)
            dlast.append(jnp.where(place == 0, inner, 0.0))
            dstate = (last_now * dstate + given - nn(transfer, dstate)) * (1.0 - reset_now)
        joined = [jnp.concatenate(p[::-1], 0) for p in (dupdates, dsolved_k, dquery, dkey, dlast)]
        dq, dk, dv, dbeta, dlog = pull_intra(
            (joined[0], joined[1], dscores, joined[2], joined[3], joined[4])
        )
        dsmall_ref[span, 0:1] = dbeta * beta * (1.0 - beta)
        dshift = dlog * (-jnp.exp(alog_ref[...])) * lax.logistic(shifted)
        dsmall_ref[span, 1:2] = dshift
        dalog = dalog + jnp.sum(dlog * log_decay, 0, keepdims=True)
        dbias = dbias + jnp.sum(dshift, 0, keepdims=True)
        slope = gate_of * (1.0 + summed * (1.0 - gate_of))
        dpadded[span, :] = jnp.concatenate([dq, dk, dv], 1) * slope
    for first in range(0, length, SUPER):
        span = slice(first, first + SUPER)
        here = dpadded[span, :]
        total = conv_ref[0:1, :] * here
        dconv[0] = dconv[0] + jnp.sum(here * padded[pl.ds(8 + first, SUPER), :], 0, keepdims=True)
        place = lax.broadcasted_iota(jnp.int32, (SUPER, 1), 0)
        at_last = place >= SUPER - 8
        for offset in range(1, tap_count):
            back = padded[pl.ds(8 + first - offset, SUPER), :] * taps_kept(reset_ref[span, :], offset)
            dconv[offset] = dconv[offset] + jnp.sum(here * back, 0, keepdims=True)
            ahead = dpadded[pl.ds(first + offset, SUPER), :]
            kept = next_kept(reset_ref, first, length, offset)
            total = total + conv_ref[offset : offset + 1, :] * (ahead * kept)
        dproj_ref[span, :channels] = total.astype(dproj_ref.dtype)
    for offset in range(tap_count):
        dconv_ref[offset : offset + 1, :] = dconv[offset]
    dalog_ref[...] = dalog
    dbias_ref[...] = dbias
    dgain_ref[...] = dgain


def next_kept(reset_ref, first, length, offset):
    place = lax.broadcasted_iota(jnp.int32, (BLOCK, 1), 0)
    kept = []
    for start in range(first, first + SUPER, BLOCK):
        if start + BLOCK < length:
            after = 1.0 - reset_ref[start + BLOCK : start + 2 * BLOCK, :]
        else:
            after = jnp.zeros((BLOCK, 1), jnp.float32)
        kept.append(jnp.where(place + offset >= BLOCK, after, 1.0))
    return jnp.concatenate(kept, 0)


vmem_limit = 60 * 1024 * 1024


def run_kernel(kernel, out_shape, scratch, operands, cost):
    return pl.pallas_call(
        kernel,
        out_shape=out_shape,
        in_specs=[pl.BlockSpec(memory_space=pltpu.VMEM)] * len(operands),
        out_specs=[pl.BlockSpec(memory_space=pltpu.VMEM)] * len(out_shape),
        scratch_shapes=scratch,
        compiler_params=pltpu.CompilerParams(vmem_limit_bytes=vmem_limit),
        cost_estimate=pl.CostEstimate(flops=cost, bytes_accessed=8_000_000, transcendentals=1_000_000),
    )(*operands)


def head_forward(operands):
    projected, conv, gain = operands[0], operands[3], operands[6]
    length, value_width = projected.shape[0], gain.shape[1]
    key_width = (conv.shape[1] - value_width) // 2
    f32 = jnp.float32
    out_shape = [
        jax.ShapeDtypeStruct((length, value_width), jnp.bfloat16),
        jax.ShapeDtypeStruct((length, value_width), f32),
        jax.ShapeDtypeStruct((length, SUPER), f32),
        jax.ShapeDtypeStruct((length // BLOCK * key_width, value_width), f32),
        jax.ShapeDtypeStruct((length, value_width), f32),
    ]
    scratch = [pltpu.VMEM((length + 8, conv.shape[1]), f32)]
    return run_kernel(forward_kernel, out_shape, scratch, operands, 20_000_000_000)


def head_backward(operands, kept, grad_mixed):
    projected, small, conv, gain = operands[0], operands[1], operands[3], operands[6]
    f32 = jnp.float32
    out_shape = [
        jax.ShapeDtypeStruct(projected.shape, jnp.bfloat16),
        jax.ShapeDtypeStruct(small.shape, f32),
        jax.ShapeDtypeStruct(conv.shape, f32),
        jax.ShapeDtypeStruct((1, 1), f32),
        jax.ShapeDtypeStruct((1, 1), f32),
        jax.ShapeDtypeStruct(gain.shape, f32),
    ]
    scratch = [pltpu.VMEM((projected.shape[0] + 8, conv.shape[1]), f32)] * 2
    return run_kernel(
        backward_kernel, out_shape, scratch, (*operands, *kept, grad_mixed), 40_000_000_000
    )


def row_total(partial_rows):
    return lax.psum(partial_rows, "row")


def gather_tokens(block_rows):
    return lax.all_gather(block_rows, "col", axis=0, tiled=True)


def scatter_tokens(partial_rows):
    return lax.psum_scatter(
        partial_rows.astype(jnp.bfloat16), "col", scatter_dimension=0, tiled=True
    ).astype(jnp.float32)


def scatter_row(partial_rows):
    return lax.psum_scatter(
        partial_rows.astype(jnp.bfloat16), "row", scatter_dimension=0, tiled=True
    ).astype(jnp.float32)


def gather_row(rows):
    return lax.all_gather(rows, "row", axis=0, tiled=True)


def tie(*arrays):
    return lax.optimization_barrier(arrays)


def norm_forward(residual, gain_row, model_width):
    inverse = lax.rsqrt(row_total(jnp.sum(residual * residual, -1)) / model_width + norm_eps)
    scaled = residual * inverse[:, None]
    return (scaled * gain_row, scaled, inverse)


def norm_backward(grad_normed, scaled, inverse, gain_row, model_width):
    grad_scaled = grad_normed * gain_row
    inner_mean = row_total(jnp.sum(grad_scaled * scaled, -1)) / model_width
    grad_rows = inverse[:, None] * (grad_scaled - scaled * inner_mean[:, None])
    grad_gain = jnp.sum(grad_normed * scaled, 0)
    return (grad_rows, grad_gain)


def halving_total(part, order, size):
    index = lax.axis_index("dp")
    current = part
    for bit in order:
        upper = (index & bit) > 0
        half = current.shape[0] // 2
        low, high = current[:half], current[half:]
        away = jnp.where(upper, low, high).astype(jnp.bfloat16)
        stay = jnp.where(upper, high, low)
        came = lax.ppermute(away, "dp", [(i, i ^ bit) for i in range(size)])
        current = stay.astype(jnp.float32) + came.astype(jnp.float32)
    current = current.astype(jnp.bfloat16)
    for bit in reversed(order):
        upper = (index & bit) > 0
        came = lax.ppermute(current, "dp", [(i, i ^ bit) for i in range(size)])
        current = jnp.where(
            upper, jnp.concatenate([came, current], 0), jnp.concatenate([current, came], 0)
        )
    return current.astype(jnp.float32)


def dp_total(grad):
    size = lax.axis_size("dp")
    bits = [1 << place for place in range(size.bit_length() - 1)]
    half = grad.shape[0] // 2
    return jnp.concatenate(
        [halving_total(grad[:half], bits, size), halving_total(grad[half:], bits[::-1], size)], 0
    )


def body(
    inputs, norm_in, w_proj, w_small, w_conv, a_log, dt_bias, norm_out, w_out, norm_ffn,
    w_gu, w_down, block_resets, cotangent,
):
    row_width = norm_in.shape[1]
    row_size = lax.axis_size("row")
    col_size = lax.axis_size("col")
    model_width = row_width * row_size
    heads_col = w_proj.shape[2]
    heads_dev = heads_col // row_size
    row_index = lax.axis_index("row")
    col_index = lax.axis_index("col")
    head_first = row_index * heads_dev
    reset_tokens = jnp.repeat(block_flags(block_resets), BLOCK).astype(jnp.float32)[:, None]

    residual = inputs.astype(jnp.float32)
    normed, scaled_in, inverse_in = norm_forward(residual, norm_in[0], model_width)
    gathered_in = gather_tokens(normed.astype(jnp.bfloat16))
    length = gathered_in.shape[0]
    proj_part = jnp.einsum(
        "td,dhp->htp", gathered_in, w_proj[0], preferred_element_type=jnp.float32
    )
    small_part = jnp.einsum(
        "td,dhp->thp", gathered_in, w_small[0], preferred_element_type=jnp.float32
    )
    projected = scatter_row(proj_part)
    small_proj = lax.psum_scatter(small_part, "row", scatter_dimension=1, tiled=True)
    projected, cotangent_late = tie(projected, cotangent)
    conv_mine = lax.dynamic_slice_in_dim(w_conv[0], head_first, heads_dev, 1)
    alog_mine = lax.dynamic_slice_in_dim(a_log[0], head_first, heads_dev, 0)
    bias_mine = lax.dynamic_slice_in_dim(dt_bias[0], head_first, heads_dev, 0)
    head_args, head_kept, head_mixed = [], [], []
    for head in range(heads_dev):
        operands = (
            projected[head],
            small_proj[:, head],
            reset_tokens,
            conv_mine[:, head],
            alog_mine[head].reshape(1, 1),
            bias_mine[head].reshape(1, 1),
            norm_out,
        )
        mixed, *kept = head_forward(operands)
        head_args.append(operands)
        head_kept.append(kept)
        head_mixed.append(mixed)
    mixed_out = jnp.stack(head_mixed, 0)
    grad_branch = gather_tokens(cotangent_late)
    mixed_out, grad_branch = tie(mixed_out, grad_branch)
    gathered_heads = gather_row(mixed_out)
    branch = scatter_tokens(
        jnp.einsum("htv,hvd->td", gathered_heads, w_out[0], preferred_element_type=jnp.float32)
    )
    grad_hidden = scatter_row(
        jnp.einsum("td,fd->tf", grad_branch, w_down[0], preferred_element_type=jnp.float32)
    )
    middle = residual + branch
    normed_ffn, scaled_ffn, inverse_ffn = norm_forward(middle, norm_ffn[0], model_width)
    gathered_ffn = gather_tokens(normed_ffn.astype(jnp.bfloat16))
    gate_up = scatter_row(
        jnp.einsum("td,dkf->tkf", gathered_ffn, w_gu[0], preferred_element_type=jnp.float32)
    )
    gate_rows = gate_up[:, 0]
    up_rows = gate_up[:, 1]
    sigmoid_gate = jax.nn.sigmoid(gate_rows)
    hidden = (gate_rows * sigmoid_gate * up_rows).astype(jnp.bfloat16)
    grad_gate = grad_hidden * up_rows * sigmoid_gate * (1.0 + gate_rows * (1.0 - sigmoid_gate))
    grad_up = grad_hidden * gate_rows * sigmoid_gate
    grad_gate_up = gather_row(jnp.stack([grad_gate, grad_up], 1).astype(jnp.bfloat16))
    grad_normed_ffn = scatter_tokens(
        jnp.einsum("tkf,dkf->td", grad_gate_up, w_gu[0], preferred_element_type=jnp.float32)
    )
    hidden, _ = tie(hidden, grad_gate_up)
    hidden_all = gather_row(hidden)
    grad_down = jnp.einsum(
        "tf,td->fd", hidden_all, grad_branch, preferred_element_type=jnp.float32
    )
    grad_gu = jnp.einsum(
        "td,tkf->kfd", gathered_ffn, grad_gate_up, preferred_element_type=jnp.float32
    )
    total_down = dp_total(grad_down)
    total_gu = dp_total(grad_gu.reshape(-1, row_width))

    grad_middle, grad_gain_ffn = norm_backward(
        grad_normed_ffn, scaled_ffn, inverse_ffn, norm_ffn[0], model_width
    )
    grad_middle = cotangent.astype(jnp.float32) + grad_middle
    grad_middle_all = gather_tokens(grad_middle.astype(jnp.bfloat16))
    grad_mixed = lax.psum_scatter(
        jnp.einsum(
            "td,hvd->htv", grad_middle_all, w_out[0], preferred_element_type=jnp.float32
        ).astype(jnp.bfloat16),
        "row",
        scatter_dimension=0,
        tiled=True,
    )
    hidden_late, grad_mixed = tie(hidden_all, grad_mixed)
    last_branch = scatter_tokens(
        jnp.dot(hidden_late, w_down[0], preferred_element_type=jnp.float32)
    )
    result = (middle + last_branch).astype(jnp.bfloat16)
    grad_out = jnp.einsum(
        "htv,td->hvd", gathered_heads, grad_middle_all, preferred_element_type=jnp.float32
    )
    value_width = grad_out.shape[1]
    total_out = dp_total(grad_out.reshape(-1, row_width))

    backs = [
        head_backward(head_args[head], head_kept[head], grad_mixed[head])
        for head in range(heads_dev)
    ]
    grad_proj_mine = jnp.stack([back[0] for back in backs], 0)
    grad_small_mine = jnp.stack([back[1] for back in backs], 0).astype(jnp.bfloat16)
    grad_proj_all = gather_row(grad_proj_mine)
    grad_small_all = gather_row(grad_small_mine)
    grad_normed_in = scatter_tokens(
        jnp.einsum("htp,dhp->td", grad_proj_all, w_proj[0], preferred_element_type=jnp.float32)
        + jnp.einsum("htp,dhp->td", grad_small_all, w_small[0], preferred_element_type=jnp.float32)
    )
    grad_proj = jnp.einsum(
        "td,htp->hpd", gathered_in, grad_proj_all, preferred_element_type=jnp.float32
    )
    grad_small = jnp.einsum(
        "td,htp->hpd", gathered_in, grad_small_all, preferred_element_type=jnp.float32
    )
    proj_width = grad_proj.shape[1]
    total_proj = dp_total(grad_proj.reshape(-1, row_width))
    taps, channels = w_conv.shape[1], w_conv.shape[3]
    lanes = 128

    def padded_lanes(array):
        flat = array.reshape(-1)
        return jnp.pad(flat, (0, -flat.shape[0] % lanes)).reshape(-1, lanes)

    pieces = [
        padded_lanes(jnp.stack([back[2] for back in backs], 1)),
        padded_lanes(jnp.stack([back[3].reshape(()) for back in backs])),
        padded_lanes(jnp.stack([back[4].reshape(()) for back in backs])),
        padded_lanes(sum(back[5] for back in backs)),
        padded_lanes(grad_gain_ffn),
        padded_lanes(grad_small),
    ]
    starts = [0]
    for piece in pieces:
        starts.append(starts[-1] + piece.shape[0])
    summed = lax.psum(jnp.concatenate(pieces, 0), "dp")
    shared = lax.all_gather(summed[: starts[5]], ("col", "row"), axis=0, tiled=False)
    shared = shared.reshape(col_size, row_size, starts[5], lanes)
    mine = lax.dynamic_index_in_dim(shared, col_index, 0, keepdims=False)

    def taken(array, place, count):
        flat = array[..., starts[place] : starts[place + 1], :]
        return flat.reshape(flat.shape[:-2] + (-1,))[..., :count]

    conv_rows = taken(mine, 0, taps * heads_dev * channels).reshape(
        row_size, taps, heads_dev, channels
    )
    grad_conv = conv_rows.transpose(1, 0, 2, 3).reshape(1, taps, heads_col, channels)
    grad_alog = taken(mine, 1, heads_dev).reshape(1, heads_col)
    grad_bias = taken(mine, 2, heads_dev).reshape(1, heads_col)
    grad_norm_out = taken(shared, 3, value_width).sum((0, 1))[None]
    ffn_rows = taken(shared, 4, row_width).sum(0)
    grad_norm_ffn = lax.dynamic_slice_in_dim(ffn_rows, row_index, 1, 0)
    total_small = taken(summed, 5, grad_small.size).reshape(grad_small.shape)

    grad_in, grad_gain_in = norm_backward(
        grad_normed_in, scaled_in, inverse_in, norm_in[0], model_width
    )
    grad_rows = grad_middle + grad_in
    grad_norm_in = lax.psum(grad_gain_in, ("dp", "col"))[None]
    return (
        result,
        grad_rows,
        grad_norm_in,
        total_proj.reshape(heads_col, proj_width, row_width).transpose(2, 0, 1)[None],
        total_small.transpose(2, 0, 1)[None],
        grad_conv,
        grad_alog,
        grad_bias,
        grad_norm_out,
        total_out.reshape(heads_col, value_width, row_width)[None],
        grad_norm_ffn,
        total_gu.reshape(w_gu.shape[2], w_gu.shape[3], row_width).transpose(2, 0, 1)[None],
        total_down[None],
    )


def solution(mesh):
    in_specs = (
        P(("dp", "col"), "row"),
        P(None, "row"),
        P(None, "row", "col", None),
        P(None, "row", "col", None),
        P(None, None, "col", None),
        P(None, "col"),
        P(None, "col"),
        P(),
        P(None, "col", None, "row"),
        P(None, "row"),
        P(None, "row", None, "col"),
        P(None, "col", "row"),
        P("dp", None),
        P(("dp", "col"), "row"),
    )
    out_specs = (
        P(("dp", "col"), "row"),
        P(("dp", "col"), "row"),
        P(None, "row"),
        P(None, "row", "col", None),
        P(None, "row", "col", None),
        P(None, None, "col", None),
        P(None, "col"),
        P(None, "col"),
        P(),
        P(None, "col", None, "row"),
        P(None, "row"),
        P(None, "row", None, "col"),
        P(None, "col", "row"),
    )
    return jax.shard_map(body, mesh=mesh, in_specs=in_specs, out_specs=out_specs, check_vma=False)
```

time: 1460 us -> 536 us (0.37)
  other arithmetic: 434 us -> 47.5 us
  waiting for transfers between devices: 516 us -> 232 us
  matrix products: 252 us -> 46.2 us
  local copies, waits for them, and re-layouts: 132 us -> 18.8 us
  Pallas kernels: 0 us -> 52.5 us
  starting transfers between devices: 1.14 us -> 37.9 us
  loops' own time: 23.7 us -> 0 us
    another operation x200 -> x1, other arithmetic: 289 us -> 1.1 us  [body(): total_out.reshape(heads_col, value_width, row_width)[None]]
    psum x2 -> x0, waiting for transfers between devices: 199 us -> none  [the longest x1 104 us: reduce_mixer(): lax.psum(grad_proj.astype(jnp.bfloat16), 'dp').astype(jnp.float32)]
    dot_general x366 -> x14, matrix products: 231 us -> 43.5 us  [the longest x1 5.02 us: body(): jnp.einsum('tkf,dkf->td', grad_gate_up, w_gu[0], preferred_element_type=j...]
    reduce_scatter x8 -> x9, waiting for transfers between devices: 171 us -> 86.6 us  [the longest x4 56.8 us: scatter_tokens(): lax.psum_scatter(partial_rows.astype(jnp.bfloat16), 'col', scatter_dimens...]
    pallas_call x0 -> x2, Pallas kernels: none -> 52.5 us  [run_kernel(): pl.pallas_call(kernel, out_shape=out_shape, in_specs=[pl.BlockSpec(memory...]
    ppermute x0 -> x32, waiting for transfers between devices: none -> 51.4 us  [the longest x16 26.6 us: halving_total(): came = lax.ppermute(current, 'dp', [(i, i ^ bit) for i in range(size)])]
    mul x86 -> x0, other arithmetic: 47.3 us -> none  [the longest x48 14.7 us: block_step(): (beta_rows * decays)[:, None] * keys_now]
    slice x66 -> x4, local copies, waits for them, and re-layouts: 38.7 us -> 0.08 us  [the longest x3 0.07 us: taken(): flat = array[..., starts[place]:starts[place + 1], :]]
  transfers between devices with their start and end apart: 18 -> 49, of which waited for: 17 -> 35; matrix products, arithmetic and copies ran while one was open for 4% -> 14% of each run, Pallas kernels for 0% -> 10%
where the time goes in v1:
time: 536 us; the launch traced here: 532 us
  waiting for transfers between devices  232 us (43%)
  blocking collectives  81.6 us (15%)
  Pallas kernels  52.5 us (10%)
  other arithmetic  47.5 us (9%)
  matrix products  46.2 us (9%)
  starting transfers between devices  37.9 us (7%)
  local copies, waits for them, and re-layouts  18.8 us (4%)
  between operations  15 us (3%)
    all_gather x4, waiting for transfers between devices, gather_tokens(): return lax.all_gather(block_rows, 'col', axis=0, tiled=True)  69.7 us
    reduce_scatter x4, waiting for transfers between devices, scatter_tokens(): lax.psum_scatter(partial_rows.astype(jnp.bfloat16), 'col', scatter_dimens...  56.8 us
    pallas_call x2, Pallas kernels, run_kernel(): pl.pallas_call(kernel, out_shape=out_shape, in_specs=[pl.BlockSpec(memory...  52.5 us
    psum x1, blocking collectives, body(): grad_norm_in = lax.psum(grad_gain_in, ('dp', 'col'))[None]  40 us
    ppermute x16, waiting for transfers between devices, halving_total(): came = lax.ppermute(current, 'dp', [(i, i ^ bit) for i in range(size)])  26.6 us
    ppermute x16, waiting for transfers between devices, halving_total(): came = lax.ppermute(away, 'dp', [(i, i ^ bit) for i in range(size)])  24.8 us
    all_gather x4, waiting for transfers between devices, gather_row(): return lax.all_gather(rows, 'row', axis=0, tiled=True)  23.5 us
    reduce_scatter x3, waiting for transfers between devices, scatter_row(): lax.psum_scatter(partial_rows.astype(jnp.bfloat16), 'row', scatter_dimens...  20.7 us
  transfers between devices with their start and end apart: 49, of which 35 were waited for; matrix products, arithmetic and copies ran while one was open for 14% of the time, Pallas kernels for 10%

profile of v1, /device:TPU:0, one launch (start us, length us, event | category | flops | bytes accessed | tf_op | source)
XLA Modules:
  0.0 531.6 jit_solution(16124176158767099531)
XLA Ops:
  8.4 2.6 psum.42
  12.9 30.6 %all-gather.12.cloned.1.call-done = bf16[1024,512]{1,0:T(8,128)(2,1)} async-done(((bf16[256,512]{1,0:T(8,128)(2,1)}), bf16[1024,512]{1,0:T(8,128)(2,1)}) %all-gather.12.cloned.1.call-update) | async-done | bytes 1048592 | tf_op jit(solution)/shard_map/all_gather | solution.py:368
  43.5 4.7 convert_bitcast_fusion
  53.5 5.3 reduce-scatter.10.cloned.1.call-done
  58.8 3.3 convert_element_type.249
  62.4 9.1 %reduce-scatter.12.cloned.1.call-done = f32[1024,1,2]{2,0,1:T(8,128)} async-done(((f32[1024,2,2]{2,0,1:T(8,128)}), f32[1024,1,2]{2,0,1:T(8,128)}) %reduce-scatter.12.cloned.1.call-update) | async-done | bytes 8208 | tf_op jit(solution)/shard_map/reduce_scatter | solution.py:461
  71.4 24.8 %shard_map.237 = (bf16[1024,256]{1,0:T(8,128)(2,1)}, f32[1024,256]{1,0:T(8,128)}, f32[1024,256]{1,0:T(8,128)}, f32[2048,256]{1,0:T(8,128)}, f32[1024,256]{1,0:T(8,128)}) custom-call(f32[1024,768]{1,0:T(8,128)} %bitcast.185, f32[1024,2]{1,0:T(8,128)} %bitcast.212, f32[1024,1]{1,0:T(8,128)} %convert_element_type.320.reset_ref, f32[4,512]{1,0:T(4,128)} %bitcast.205, ...), custom_call_target="tpu_custom_call" | custom-call | flops 20000000000 | bytes 8000000 | tf_op jit(solution)/shard_map/pallas_call | solution.py:319
  96.3 5.7 %all-gather.14.cloned.1.call-done = bf16[1024,512]{1,0:T(8,128)(2,1)} async-done(((bf16[256,512]{1,0:T(8,128)(2,1)}), bf16[1024,512]{1,0:T(8,128)(2,1)}) %all-gather.14.cloned.1.call-update) | async-done | bytes 1048592 | tf_op jit(solution)/shard_map/all_gather | solution.py:368
  102.1 10.4 %all-gather.16.cloned.1.call-done = bf16[2,1024,256]{2,1,0:T(8,128)(2,1)} async-done(((bf16[1,1024,256]{2,1,0:T(8,128)(2,1)}), bf16[2,1024,256]{2,1,0:T(8,128)(2,1)}) %all-gather.16.cloned.1.call-update) | async-done | bytes 1048592 | tf_op jit(solution)/shard_map/all_gather | solution.py:384
  112.5 2.9 bitcast_convert_fusion.1
  115.5 28.4 %reduce-scatter.14.cloned.1.call-done = bf16[256,512]{1,0:T(8,128)(2,1)} async-done(((bf16[1024,512]{1,0:T(8,128)(2,1)}), bf16[256,512]{1,0:T(8,128)(2,1)}) %reduce-scatter.14.cloned.1.call-update) | async-done | bytes 262160 | tf_op jit(solution)/shard_map/reduce_scatter | solution.py:372
  145.0 2.5 psum.43
  149.4 26.7 %all-gather.18.cloned.1.call-done = bf16[1024,512]{1,0:T(8,128)(2,1)} async-done(((bf16[256,512]{1,0:T(8,128)(2,1)}), bf16[1024,512]{1,0:T(8,128)(2,1)}) %all-gather.18.cloned.1.call-update) | async-done | bytes 1048592 | tf_op jit(solution)/shard_map/all_gather | solution.py:368
  176.0 5.0 convolution_convert_fusion
  182.2 3.2 convolution_convert_fusion.1
  185.4 5.7 %reduce-scatter.16.cloned.1.call-done = bf16[512,2,704]{0,2,1:T(8,128)(2,1)} async-done(((bf16[1024,2,704]{0,2,1:T(8,128)(2,1)}), bf16[512,2,704]{0,2,1:T(8,128)(2,1)}) %reduce-scatter.16.cloned.1.call-update) | async-done | bytes 1441808 | tf_op jit(solution)/shard_map/reduce_scatter | solution.py:378
  191.2 3.3 convert_element_type.257
  194.5 9.7 %reduce-scatter.18.cloned.1.call-done = bf16[512,704]{0,1:T(8,128)(2,1)} async-done(((bf16[1024,704]{0,1:T(8,128)(2,1)}), bf16[512,704]{0,1:T(8,128)(2,1)}) %reduce-scatter.18.cloned.1.call-update) | async-done | bytes 720912 | tf_op jit(solution)/shard_map/reduce_scatter | solution.py:378
  204.2 3.6 fusion.33
  209.1 13.0 %all-gather.20.cloned.1.call-done = bf16[1024,2,704]{0,2,1:T(8,128)(2,1)} async-done(((bf16[512,2,704]{0,2,1:T(8,128)(2,1)}), bf16[1024,2,704]{0,2,1:T(8,128)(2,1)}) %all-gather.20.cloned.1.call-update) | async-done | bytes 2883600 | tf_op jit(solution)/shard_map/all_gather | solution.py:384
  222.2 5.0 bitcast_convert_fusion
  227.3 28.4 %reduce-scatter.20.cloned.1.call-done = bf16[256,512]{1,0:T(8,128)(2,1)} async-done(((bf16[1024,512]{1,0:T(8,128)(2,1)}), bf16[256,512]{1,0:T(8,128)(2,1)}) %reduce-scatter.20.cloned.1.call-update) | async-done | bytes 262160 | tf_op jit(solution)/shard_map/reduce_scatter | solution.py:372
  257.0 2.5 psum.44
  262.1 3.5 fusion.15
  268.8 7.5 %collective-permute-done.16 = bf16[352,512]{1,0:T(8,128)(2,1)S(1)} collective-permute-done((bf16[352,512]{1,0:T(8,128)(2,1)S(1)}, bf16[352,512]{1,0:T(8,128)(2,1)S(1)}, u32[]{:S(2)}, u32[]{:S(2)}) %collective-permute-start.16) | collective-permute-done | bytes 360480 | tf_op jit(solution)/shard_map/ppermute | solution.py:414
  281.4 6.7 %all-gather.24.cloned.1.call-done = bf16[1024,512]{1,0:T(8,128)(2,1)} async-done(((bf16[256,512]{1,0:T(8,128)(2,1)}), bf16[1024,512]{1,0:T(8,128)(2,1)}) %all-gather.24.cloned.1.call-update) | async-done | bytes 1048592 | tf_op jit(solution)/shard_map/all_gather | solution.py:368
  288.1 3.1 fusion.11
  296.5 2.1 collective-permute-done.22
  301.9 6.7 %collective-permute-done.23 = bf16[352,512]{1,0:T(8,128)(2,1)S(1)} collective-permute-done((bf16[352,512]{1,0:T(8,128)(2,1)S(1)}, bf16[352,512]{1,0:T(8,128)(2,1)S(1)}, u32[]{:S(2)}, u32[]{:S(2)}) %collective-permute-start.23) | collective-permute-done | bytes 360480 | tf_op jit(solution)/shard_map/ppermute | solution.py:419
  310.3 2.6 fusion.61
  316.9 27.7 %shard_map.238 = (bf16[1024,768]{1,0:T(8,128)(2,1)}, f32[1024,2]{1,0:T(8,128)}, f32[4,512]{1,0:T(4,128)}, f32[1,1]{1,0:T(1,128)}, f32[1,1]{1,0:T(1,128)}, /*index=5*/f32[1,256]{1,0:T(1,128)}) custom-call(f32[1024,768]{1,0:T(8,128)} %bitcast.186, f32[1024,2]{1,0:T(8,128)} %bitcast.213, f32[1024,1]{1,0:T(8,128)} %convert_element_type.320.reset_ref, ...), custom_call_target="tpu_custom_call" | custom-call | flops 40000000000 | bytes 8000000 | tf_op jit(solution)/shard_map/pallas_call | solution.py:319
  350.3 3.0 collective-permute-done.29
  355.8 2.8 collective-permute-done.30
  372.1 2.2 all-gather.1
  374.3 3.7 fusion.8
  388.4 2.3 fusion.29
  395.8 15.4 %psum.47 = f32[40,128]{1,0:T(8,128)S(1)} all-reduce(f32[40,128]{1,0:T(8,128)S(1)} %concatenate.124), channel_id=1, replica_groups=mesh['dp'=4,'row'=2,'col'=4] {'dp'}, use_global_device_ids=true, to_apply=%region_20.21 | all-reduce | flops 5120 | bytes 40960 | tf_op jit(solution)/shard_map/psum | solution.py:580
  411.3 13.9 %all-gather.2 = f32[192,128]{1,0:T(8,128)S(1)} all-gather(f32[24,128]{1,0:T(8,128)S(1)} %slice.225), channel_id=4, replica_groups=mesh['dp'=4,'row'=2,'col'=4] {'col','row'}, dimensions={0}, use_global_device_ids=true | all-gather | bytes 110592 | tf_op jit(solution)/shard_map/all_gather | solution.py:581
  426.9 3.6 convolution_convert_fusion.2
  430.6 3.7 fusion.20
  437.2 8.7 %collective-permute-done = bf16[384,512]{1,0:T(8,128)(2,1)S(1)} collective-permute-done((bf16[384,512]{1,0:T(8,128)(2,1)S(1)}, bf16[384,512]{1,0:T(8,128)(2,1)S(1)}, u32[]{:S(2)}, u32[]{:S(2)}) %collective-permute-start) | collective-permute-done | bytes 393248 | tf_op jit(solution)/shard_map/ppermute | solution.py:414
  449.7 3.2 collective-permute-done.5
  456.6 2.1 collective-permute-done.6
  466.1 2.8 collective-permute-done.7
  473.4 5.2 copy.56
  479.8 2.5 psum.45
  482.3 40.0 %psum.46 = f32[1,512]{1,0:T(1,128)} all-reduce(f32[1,512]{1,0:T(1,128)S(1)} %bitcast.204), channel_id=1, replica_groups=mesh['dp'=4,'row'=2,'col'=4] {'dp','col'}, use_global_device_ids=true, to_apply=%region_18.19 | all-reduce | flops 512 | bytes 4096 | tf_op jit(solution)/shard_map/psum | solution.py:604
  522.3 2.3 fusion.38
  (251 shorter events, 102.8 us)
Async XLA Ops:
  7.2 36.3 %all-gather.12.cloned.1.call-start = ((), (), s32[]{:S(2)}) async-start(), calls=%async_computation.9 | async-start | bytes 1310720 | tf_op jit(solution)/shard_map/all_gather | solution.py:368
  12.8 45.9 %reduce-scatter.10.cloned.1.call-start = ((), (), s32[]{:S(2)}) async-start(), calls=%async_computation.10 | async-start | bytes 4718592 | tf_op jit(solution)/shard_map/reduce_scatter | solution.py:378
  48.2 23.2 %reduce-scatter.12.cloned.1.call-start = ((), (), s32[]{:S(2)}) async-start(), calls=%async_computation.11 | async-start | bytes 1572864 | tf_op jit(solution)/shard_map/reduce_scatter | solution.py:461
  50.9 51.1 %all-gather.14.cloned.1.call-start = ((), (), s32[]{:S(2)}) async-start(), calls=%async_computation.12 | async-start | bytes 1310720 | tf_op jit(solution)/shard_map/all_gather | solution.py:368
  62.1 50.4 %all-gather.16.cloned.1.call-start = ((), (), s32[]{:S(2)}) async-start(), calls=%async_computation.13 | async-start | bytes 1572864 | tf_op jit(solution)/shard_map/all_gather | solution.py:384
  102.0 41.9 %reduce-scatter.14.cloned.1.call-start = ((), (), s32[]{:S(2)}) async-start(), calls=%async_computation.14 | async-start | bytes 1310720 | tf_op jit(solution)/shard_map/reduce_scatter | solution.py:372
  115.4 60.6 %all-gather.18.cloned.1.call-start = ((), (), s32[]{:S(2)}) async-start(), calls=%async_computation.15 | async-start | bytes 1310720 | tf_op jit(solution)/shard_map/all_gather | solution.py:368
  149.3 41.8 %reduce-scatter.16.cloned.1.call-start = ((), (), s32[]{:S(2)}) async-start(), calls=%async_computation.16 | async-start | bytes 4325376 | tf_op jit(solution)/shard_map/reduce_scatter | solution.py:378
  181.0 23.2 %reduce-scatter.18.cloned.1.call-start = ((), (), s32[]{:S(2)}) async-start(), calls=%async_computation.17 | async-start | bytes 2162688 | tf_op jit(solution)/shard_map/reduce_scatter | solution.py:378
  185.4 36.8 %all-gather.20.cloned.1.call-start = ((), (), s32[]{:S(2)}) async-start(), calls=%async_computation.18 | async-start | bytes 4325376 | tf_op jit(solution)/shard_map/all_gather | solution.py:384
  209.1 46.6 %reduce-scatter.20.cloned.1.call-start = ((), (), s32[]{:S(2)}) async-start(), calls=%async_computation.20 | async-start | bytes 1310720 | tf_op jit(solution)/shard_map/reduce_scatter | solution.py:372
  227.3 60.8 %all-gather.24.cloned.1.call-start = ((), (), s32[]{:S(2)}) async-start(), calls=%async_computation.21 | async-start | bytes 1310720 | tf_op jit(solution)/shard_map/all_gather | solution.py:368
  261.3 48.9 %all-gather.22.cloned.1.call-start = ((), (), s32[]{:S(2)}) async-start(), calls=%async_computation.19 | async-start | bytes 2162688 | tf_op jit(solution)/shard_map/all_gather | solution.py:384
  262.1 54.8 %reduce-scatter.22.cloned.1.call-start = ((), (), s32[]{:S(2)}) async-start(), calls=%async_computation.22 | async-start | bytes 1572864 | tf_op jit(solution)/shard_map/reduce_scatter | solution.py:523
  265.8 10.6 %collective-permute-start.16 = (bf16[352,512]{1,0:T(8,128)(2,1)S(1)}, bf16[352,512]{1,0:T(8,128)(2,1)S(1)}, u32[]{:S(2)}, u32[]{:S(2)}) collective-permute-start(bf16[352,512]{1,0:T(8,128)(2,1)S(1)} %get-tuple-element.87), channel_id=1, source_target_pairs={{0,8},{8,0},{16,24},{24,16},{1,9},{9,1},{17,25},{25,17},{2,10},{10... | collective-permute-start | bytes 1081352 | tf_op jit(solution)/shard_map/ppermute | solution.py:414
  267.3 10.2 %collective-permute-start.20 = (bf16[352,512]{1,0:T(8,128)(2,1)S(1)}, bf16[352,512]{1,0:T(8,128)(2,1)S(1)}, u32[]{:S(2)}, u32[]{:S(2)}) collective-permute-start(bf16[352,512]{1,0:T(8,128)(2,1)S(1)} %get-tuple-element.88), channel_id=1, source_target_pairs={{0,16},{8,24},{16,0},{24,8},{1,17},{9,25},{17,1},{25,9},{2,18},{10... | collective-permute-start | bytes 1081352 | tf_op jit(solution)/shard_map/ppermute | solution.py:414
  278.6 12.8 %collective-permute-start.21 = (bf16[176,512]{1,0:T(8,128)(2,1)}, bf16[176,512]{1,0:T(8,128)(2,1)}, u32[]{:S(2)}, u32[]{:S(2)}) collective-permute-start(bf16[176,512]{1,0:T(8,128)(2,1)} %select_convert_fusion.8), channel_id=1, source_target_pairs={{0,8},{8,0},{16,24},{24,16},{1,9},{9,1},{17,25},{25,17},{2,10},{10... | collective-permute-start | bytes 540680 | tf_op jit(solution)/shard_map/ppermute | solution.py:414
  279.9 14.1 %collective-permute-start.17 = (bf16[176,512]{1,0:T(8,128)(2,1)}, bf16[176,512]{1,0:T(8,128)(2,1)}, u32[]{:S(2)}, u32[]{:S(2)}) collective-permute-start(bf16[176,512]{1,0:T(8,128)(2,1)} %select_convert_fusion.9), channel_id=1, source_target_pairs={{0,16},{8,24},{16,0},{24,8},{1,17},{9,25},{17,1},{25,9},{2,18},{10... | collective-permute-start | bytes 540680 | tf_op jit(solution)/shard_map/ppermute | solution.py:414
  291.2 83.1 %all-gather.26.cloned.1.call-start = ((), (), s32[]{:S(2)}) async-start(), calls=%async_computation.25 | async-start | bytes 4718592 | tf_op jit(solution)/shard_map/all_gather | solution.py:384
  292.4 6.2 %collective-permute-start.22 = (bf16[176,512]{1,0:T(8,128)(2,1)S(1)}, bf16[176,512]{1,0:T(8,128)(2,1)S(1)}, u32[]{:S(2)}, u32[]{:S(2)}) collective-permute-start(bf16[176,512]{1,0:T(8,128)(2,1)S(1)} %add_convert_fusion.3), channel_id=1, source_target_pairs={{0,8},{8,0},{16,24},{24,16},{1,9},{9,1},{17,25},{25,17},{2,10},{10... | collective-permute-start | bytes 540680 | tf_op jit(solution)/shard_map/ppermute | solution.py:419
  295.0 6.6 %collective-permute-start.18 = (bf16[176,512]{1,0:T(8,128)(2,1)S(1)}, bf16[176,512]{1,0:T(8,128)(2,1)S(1)}, u32[]{:S(2)}, u32[]{:S(2)}) collective-permute-start(bf16[176,512]{1,0:T(8,128)(2,1)S(1)} %add_convert_fusion.4), channel_id=1, source_target_pairs={{0,16},{8,24},{16,0},{24,8},{1,17},{9,25},{17,1},{25,9},{2,18},{10... | collective-permute-start | bytes 540680 | tf_op jit(solution)/shard_map/ppermute | solution.py:419
  298.7 9.9 %collective-permute-start.23 = (bf16[352,512]{1,0:T(8,128)(2,1)S(1)}, bf16[352,512]{1,0:T(8,128)(2,1)S(1)}, u32[]{:S(2)}, u32[]{:S(2)}) collective-permute-start(bf16[352,512]{1,0:T(8,128)(2,1)S(1)} %maximum_select_fusion.7), channel_id=1, source_target_pairs={{0,16},{8,24},{16,0},{24,8},{1,17},{9,25},{17,1},{25,9},{2,18},{10... | collective-permute-start | bytes 1081352 | tf_op jit(solution)/shard_map/ppermute | solution.py:419
  301.6 8.2 %collective-permute-start.19 = (bf16[352,512]{1,0:T(8,128)(2,1)S(1)}, bf16[352,512]{1,0:T(8,128)(2,1)S(1)}, u32[]{:S(2)}, u32[]{:S(2)}) collective-permute-start(bf16[352,512]{1,0:T(8,128)(2,1)S(1)} %maximum_select_fusion.6), channel_id=1, source_target_pairs={{0,8},{8,0},{16,24},{24,16},{1,9},{9,1},{17,25},{25,17},{2,10},{10... | collective-permute-start | bytes 1081352 | tf_op jit(solution)/shard_map/ppermute | solution.py:419
  314.8 32.1 %collective-permute-start.24 = (bf16[176,512]{1,0:T(8,128)(2,1)}, bf16[176,512]{1,0:T(8,128)(2,1)}, u32[]{:S(2)}, u32[]{:S(2)}) collective-permute-start(bf16[176,512]{1,0:T(8,128)(2,1)} %get-tuple-element.94), channel_id=1, source_target_pairs={{0,8},{8,0},{16,24},{24,16},{1,9},{9,1},{17,25},{25,17},{2,10},{10... | collective-permute-start | bytes 540680 | tf_op jit(solution)/shard_map/ppermute | solution.py:414
  315.8 31.1 %collective-permute-start.28 = (bf16[176,512]{1,0:T(8,128)(2,1)}, bf16[176,512]{1,0:T(8,128)(2,1)}, u32[]{:S(2)}, u32[]{:S(2)}) collective-permute-start(bf16[176,512]{1,0:T(8,128)(2,1)} %get-tuple-element.95), channel_id=1, source_target_pairs={{0,16},{8,24},{16,0},{24,8},{1,17},{9,25},{17,1},{25,9},{2,18},{10... | collective-permute-start | bytes 540680 | tf_op jit(solution)/shard_map/ppermute | solution.py:414
  344.6 134.0 %reduce-scatter.26.cloned.1.call-start = ((), (), s32[]{:S(2)}) async-start(), calls=%async_computation.24 | async-start | bytes 1310720 | tf_op jit(solution)/shard_map/reduce_scatter | solution.py:372
  348.2 5.1 collective-permute-start.29
  349.8 5.4 %collective-permute-start.25 = (bf16[88,512]{1,0:T(8,128)(2,1)S(1)}, bf16[88,512]{1,0:T(8,128)(2,1)S(1)}, u32[]{:S(2)}, u32[]{:S(2)}) collective-permute-start(bf16[88,512]{1,0:T(8,128)(2,1)S(1)} %select_convert_fusion.13), channel_id=1, source_target_pairs={{0,16},{8,24},{16,0},{24,8},{1,17},{9,25},{17,1},{25,9},{2,18},{10... | collective-permute-start | bytes 270344 | tf_op jit(solution)/shard_map/ppermute | solution.py:414
  353.3 5.3 collective-permute-start.30
  355.2 4.8 collective-permute-start.26
  358.7 5.6 %collective-permute-start.31 = (bf16[176,512]{1,0:T(8,128)(2,1)S(1)}, bf16[176,512]{1,0:T(8,128)(2,1)S(1)}, u32[]{:S(2)}, u32[]{:S(2)}) collective-permute-start(bf16[176,512]{1,0:T(8,128)(2,1)S(1)} %maximum_select_fusion.13), channel_id=1, source_target_pairs={{0,16},{8,24},{16,0},{24,8},{1,17},{9,25},{17,1},{25,9},{2,18},{10... | collective-permute-start | bytes 540680 | tf_op jit(solution)/shard_map/ppermute | solution.py:419
  360.0 6.3 %collective-permute-start.27 = (bf16[176,512]{1,0:T(8,128)(2,1)S(1)}, bf16[176,512]{1,0:T(8,128)(2,1)S(1)}, u32[]{:S(2)}, u32[]{:S(2)}) collective-permute-start(bf16[176,512]{1,0:T(8,128)(2,1)S(1)} %maximum_select_fusion.12), channel_id=1, source_target_pairs={{0,8},{8,0},{16,24},{24,16},{1,9},{9,1},{17,25},{25,17},{2,10},{10... | collective-permute-start | bytes 540680 | tf_op jit(solution)/shard_map/ppermute | solution.py:419
  361.9 5.7 %collective-permute-start.8 = (bf16[128,512]{1,0:T(8,128)(2,1)S(1)}, bf16[128,512]{1,0:T(8,128)(2,1)S(1)}, u32[]{:S(2)}, u32[]{:S(2)}) collective-permute-start(bf16[128,512]{1,0:T(8,128)(2,1)S(1)} %get-tuple-element.98), channel_id=1, source_target_pairs={{0,8},{8,0},{16,24},{24,16},{1,9},{9,1},{17,25},{25,17},{2,10},{10... | collective-permute-start | bytes 393224 | tf_op jit(solution)/shard_map/ppermute | solution.py:414
  362.9 5.3 collective-permute-start.12
  369.0 10.6 %collective-permute-start.13 = (bf16[64,512]{1,0:T(8,128)(2,1)}, bf16[64,512]{1,0:T(8,128)(2,1)}, u32[]{:S(2)}, u32[]{:S(2)}) collective-permute-start(bf16[64,512]{1,0:T(8,128)(2,1)} %select_convert_fusion.14), channel_id=1, source_target_pairs={{0,8},{8,0},{16,24},{24,16},{1,9},{9,1},{17,25},{25,17},{2,10},{10... | collective-permute-start | bytes 196616 | tf_op jit(solution)/shard_map/ppermute | solution.py:414
  370.6 10.8 %collective-permute-start.9 = (bf16[64,512]{1,0:T(8,128)(2,1)}, bf16[64,512]{1,0:T(8,128)(2,1)}, u32[]{:S(2)}, u32[]{:S(2)}) collective-permute-start(bf16[64,512]{1,0:T(8,128)(2,1)} %select_convert_fusion.15), channel_id=1, source_target_pairs={{0,16},{8,24},{16,0},{24,8},{1,17},{9,25},{17,1},{25,9},{2,18},{10... | collective-permute-start | bytes 196616 | tf_op jit(solution)/shard_map/ppermute | solution.py:414
  379.6 142.7 %reduce-scatter.24.cloned.1.call-start = ((), (), s32[]{:S(2)}) async-start(), calls=%async_computation.23 | async-start | bytes 1310720 | tf_op jit(solution)/shard_map/reduce_scatter | solution.py:372
  382.2 4.4 collective-permute-start.10
  384.9 5.8 %collective-permute-start.15 = (bf16[128,512]{1,0:T(8,128)(2,1)S(1)}, bf16[128,512]{1,0:T(8,128)(2,1)S(1)}, u32[]{:S(2)}, u32[]{:S(2)}) collective-permute-start(bf16[128,512]{1,0:T(8,128)(2,1)S(1)} %maximum_select_fusion.15), channel_id=1, source_target_pairs={{0,16},{8,24},{16,0},{24,8},{1,17},{9,25},{17,1},{25,9},{2,18},{10... | collective-permute-start | bytes 393224 | tf_op jit(solution)/shard_map/ppermute | solution.py:419
  386.7 5.0 collective-permute-start.11
  434.5 11.4 %collective-permute-start = (bf16[384,512]{1,0:T(8,128)(2,1)S(1)}, bf16[384,512]{1,0:T(8,128)(2,1)S(1)}, u32[]{:S(2)}, u32[]{:S(2)}) collective-permute-start(bf16[384,512]{1,0:T(8,128)(2,1)S(1)} %get-tuple-element.83), channel_id=1, source_target_pairs={{0,8},{8,0},{16,24},{24,16},{1,9},{9,1},{17,25},{25,17},{2,10},{10... | collective-permute-start | bytes 1179656 | tf_op jit(solution)/shard_map/ppermute | solution.py:414
  434.8 11.2 %collective-permute-start.4 = (bf16[384,512]{1,0:T(8,128)(2,1)S(1)}, bf16[384,512]{1,0:T(8,128)(2,1)S(1)}, u32[]{:S(2)}, u32[]{:S(2)}) collective-permute-start(bf16[384,512]{1,0:T(8,128)(2,1)S(1)} %get-tuple-element.84), channel_id=1, source_target_pairs={{0,16},{8,24},{16,0},{24,8},{1,17},{9,25},{17,1},{25,9},{2,18},{10... | collective-permute-start | bytes 1179656 | tf_op jit(solution)/shard_map/ppermute | solution.py:414
  446.5 6.4 %collective-permute-start.5 = (bf16[192,512]{1,0:T(8,128)(2,1)S(1)}, bf16[192,512]{1,0:T(8,128)(2,1)S(1)}, u32[]{:S(2)}, u32[]{:S(2)}) collective-permute-start(bf16[192,512]{1,0:T(8,128)(2,1)S(1)} %select_convert_fusion.4), channel_id=1, source_target_pairs={{0,8},{8,0},{16,24},{24,16},{1,9},{9,1},{17,25},{25,17},{2,10},{10... | collective-permute-start | bytes 589832 | tf_op jit(solution)/shard_map/ppermute | solution.py:414
  448.2 6.3 %collective-permute-start.1 = (bf16[192,512]{1,0:T(8,128)(2,1)S(1)}, bf16[192,512]{1,0:T(8,128)(2,1)S(1)}, u32[]{:S(2)}, u32[]{:S(2)}) collective-permute-start(bf16[192,512]{1,0:T(8,128)(2,1)S(1)} %select_convert_fusion.5), channel_id=1, source_target_pairs={{0,16},{8,24},{16,0},{24,8},{1,17},{9,25},{17,1},{25,9},{2,18},{10... | collective-permute-start | bytes 589832 | tf_op jit(solution)/shard_map/ppermute | solution.py:414
  453.0 5.7 %collective-permute-start.6 = (bf16[192,512]{1,0:T(8,128)(2,1)S(1)}, bf16[192,512]{1,0:T(8,128)(2,1)S(1)}, u32[]{:S(2)}, u32[]{:S(2)}) collective-permute-start(bf16[192,512]{1,0:T(8,128)(2,1)S(1)} %add_convert_fusion.1), channel_id=1, source_target_pairs={{0,8},{8,0},{16,24},{24,16},{1,9},{9,1},{17,25},{25,17},{2,10},{10... | collective-permute-start | bytes 589832 | tf_op jit(solution)/shard_map/ppermute | solution.py:419
  454.6 6.9 %collective-permute-start.2 = (bf16[192,512]{1,0:T(8,128)(2,1)S(1)}, bf16[192,512]{1,0:T(8,128)(2,1)S(1)}, u32[]{:S(2)}, u32[]{:S(2)}) collective-permute-start(bf16[192,512]{1,0:T(8,128)(2,1)S(1)} %add_convert_fusion.2), channel_id=1, source_target_pairs={{0,16},{8,24},{16,0},{24,8},{1,17},{9,25},{17,1},{25,9},{2,18},{10... | collective-permute-start | bytes 589832 | tf_op jit(solution)/shard_map/ppermute | solution.py:419
  458.9 10.0 %collective-permute-start.7 = (bf16[384,512]{1,0:T(8,128)(2,1)S(1)}, bf16[384,512]{1,0:T(8,128)(2,1)}, u32[]{:S(2)}, u32[]{:S(2)}) collective-permute-start(bf16[384,512]{1,0:T(8,128)(2,1)S(1)} %maximum_select_fusion.5), channel_id=1, source_target_pairs={{0,16},{8,24},{16,0},{24,8},{1,17},{9,25},{17,1},{25,9},{2,18},{10... | collective-permute-start | bytes 1179656 | tf_op jit(solution)/shard_map/ppermute | solution.py:419
  462.4 8.1 %collective-permute-start.3 = (bf16[384,512]{1,0:T(8,128)(2,1)}, bf16[384,512]{1,0:T(8,128)(2,1)}, u32[]{:S(2)}, u32[]{:S(2)}) collective-permute-start(bf16[384,512]{1,0:T(8,128)(2,1)} %maximum_select_fusion.4), channel_id=1, source_target_pairs={{0,8},{8,0},{16,24},{24,16},{1,9},{9,1},{17,25},{25,17},{2,10},{10... | collective-permute-start | bytes 1179656 | tf_op jit(solution)/shard_map/ppermute | solution.py:419
  (36 other events, 772.9 us)
Sparse Core Ops, SparseCore 0:
  13.0 30.5 all-gather.11
  48.4 10.3 reduce-scatter.9
  61.7 9.6 reduce-scatter.11
  72.9 29.0 all-gather.13
  104.0 8.5 all-gather.15
  115.6 28.3 reduce-scatter.13
  149.4 26.5 all-gather.17
  181.1 9.9 reduce-scatter.15
  194.0 10.1 reduce-scatter.17
  209.2 12.9 all-gather.19
  227.4 28.2 reduce-scatter.19
  261.4 26.5 all-gather.23
  289.6 9.0 all-gather.21
  301.4 9.6 reduce-scatter.21
  344.7 11.3 all-gather.25
  379.7 25.8 reduce-scatter.25
  430.7 25.9 reduce-scatter.23

commit v2 on v1

--- a/solution.py
+++ b/solution.py
@@ -374,14 +374,41 @@
     ).astype(jnp.float32)
 
 
-def scatter_row(partial_rows):
-    return lax.psum_scatter(
-        partial_rows.astype(jnp.bfloat16), "row", scatter_dimension=0, tiled=True
-    ).astype(jnp.float32)
-
-
-def gather_row(rows):
-    return lax.all_gather(rows, "row", axis=0, tiled=True)
+def swap_row(array):
+    return lax.ppermute(array, "row", [(0, 1), (1, 0)])
+
+
+def own_half(array, index, axis=0):
+    half = array.shape[axis] // 2
+    return lax.dynamic_slice_in_dim(array, index * half, half, axis)
+
+
+def scatter_row(partial_of, index):
+    came = swap_row(partial_of(1 - index).astype(jnp.bfloat16))
+    return partial_of(index) + came.astype(jnp.float32)
+
+
+def gather_row(rows, index):
+    came = swap_row(rows)
+    return jnp.where(
+        index > 0, jnp.concatenate([came, rows], 0), jnp.concatenate([rows, came], 0)
+    )
+
+
+def spread_total(array, axis_name):
+    size = lax.axis_size(axis_name)
+    step = 1
+    while step < size:
+        count = min(4, size // step)
+        came = [array] + [
+            lax.ppermute(array, axis_name, [(i, i ^ (step * k)) for i in range(size)])
+            for k in range(1, count)
+        ]
+        array = came[0] + came[1]
+        if count == 4:
+            array = array + (came[2] + came[3])
+        step *= count
+    return array
 
 
 def tie(*arrays):
@@ -451,14 +478,18 @@
     normed, scaled_in, inverse_in = norm_forward(residual, norm_in[0], model_width)
     gathered_in = gather_tokens(normed.astype(jnp.bfloat16))
     length = gathered_in.shape[0]
-    proj_part = jnp.einsum(
-        "td,dhp->htp", gathered_in, w_proj[0], preferred_element_type=jnp.float32
-    )
+
+    def proj_part(index):
+        return jnp.einsum(
+            "td,dhp->htp", gathered_in, own_half(w_proj[0], index, 1),
+            preferred_element_type=jnp.float32,
+        )
+
     small_part = jnp.einsum(
-        "td,dhp->thp", gathered_in, w_small[0], preferred_element_type=jnp.float32
-    )
-    projected = scatter_row(proj_part)
-    small_proj = lax.psum_scatter(small_part, "row", scatter_dimension=1, tiled=True)
+        "td,dhp->htp", gathered_in, w_small[0], preferred_element_type=jnp.float32
+    )
+    projected = scatter_row(proj_part, row_index)
+    small_proj = own_half(small_part, row_index) + swap_row(own_half(small_part, 1 - row_index))
     projected, cotangent_late = tie(projected, cotangent)
     conv_mine = lax.dynamic_slice_in_dim(w_conv[0], head_first, heads_dev, 1)
     alog_mine = lax.dynamic_slice_in_dim(a_log[0], head_first, heads_dev, 0)
@@ -467,7 +498,7 @@
     for head in range(heads_dev):
         operands = (
             projected[head],
-            small_proj[:, head],
+            small_proj[head],
             reset_tokens,
             conv_mine[:, head],
             alog_mine[head].reshape(1, 1),
@@ -481,52 +512,81 @@
     mixed_out = jnp.stack(head_mixed, 0)
     grad_branch = gather_tokens(cotangent_late)
     mixed_out, grad_branch = tie(mixed_out, grad_branch)
-    gathered_heads = gather_row(mixed_out)
-    branch = scatter_tokens(
-        jnp.einsum("htv,hvd->td", gathered_heads, w_out[0], preferred_element_type=jnp.float32)
-    )
+    mixed_came = swap_row(mixed_out)
+
+    def out_part(heads, index):
+        return jnp.einsum(
+            "htv,hvd->td", heads, own_half(w_out[0], index), preferred_element_type=jnp.float32
+        )
+
+    branch_part = out_part(mixed_out, row_index) + out_part(mixed_came, 1 - row_index)
+    branch = scatter_tokens(branch_part)
+    gathered_heads = jnp.where(
+        row_index > 0,
+        jnp.concatenate([mixed_came, mixed_out], 0),
+        jnp.concatenate([mixed_out, mixed_came], 0),
+    )
+    branch_part, grad_branch_late = tie(branch_part, grad_branch)
     grad_hidden = scatter_row(
-        jnp.einsum("td,fd->tf", grad_branch, w_down[0], preferred_element_type=jnp.float32)
-    )
+        lambda index: jnp.einsum(
+            "td,fd->tf", own_half(grad_branch_late, index), w_down[0],
+            preferred_element_type=jnp.float32,
+        ),
+        row_index,
+    )
+    branch, grad_hidden = tie(branch, grad_hidden)
     middle = residual + branch
     normed_ffn, scaled_ffn, inverse_ffn = norm_forward(middle, norm_ffn[0], model_width)
     gathered_ffn = gather_tokens(normed_ffn.astype(jnp.bfloat16))
     gate_up = scatter_row(
-        jnp.einsum("td,dkf->tkf", gathered_ffn, w_gu[0], preferred_element_type=jnp.float32)
-    )
-    gate_rows = gate_up[:, 0]
-    up_rows = gate_up[:, 1]
+        lambda index: jnp.einsum(
+            "td,dkf->ktf", own_half(gathered_ffn, index), w_gu[0],
+            preferred_element_type=jnp.float32,
+        ),
+        row_index,
+    )
+    gate_rows, up_rows = gate_up[0], gate_up[1]
     sigmoid_gate = jax.nn.sigmoid(gate_rows)
     hidden = (gate_rows * sigmoid_gate * up_rows).astype(jnp.bfloat16)
     grad_gate = grad_hidden * up_rows * sigmoid_gate * (1.0 + gate_rows * (1.0 - sigmoid_gate))
     grad_up = grad_hidden * gate_rows * sigmoid_gate
-    grad_gate_up = gather_row(jnp.stack([grad_gate, grad_up], 1).astype(jnp.bfloat16))
-    grad_normed_ffn = scatter_tokens(
-        jnp.einsum("tkf,dkf->td", grad_gate_up, w_gu[0], preferred_element_type=jnp.float32)
-    )
-    hidden, _ = tie(hidden, grad_gate_up)
-    hidden_all = gather_row(hidden)
+    grad_gate_all = gather_row(grad_gate.astype(jnp.bfloat16), row_index)
+    grad_up_all = gather_row(grad_up.astype(jnp.bfloat16), row_index)
+    ffn_part = (
+        jnp.einsum("tf,df->td", grad_gate_all, w_gu[0][:, 0], preferred_element_type=jnp.float32)
+        + jnp.einsum("tf,df->td", grad_up_all, w_gu[0][:, 1], preferred_element_type=jnp.float32)
+    ).astype(jnp.bfloat16)
+    grad_normed_ffn = scatter_tokens(ffn_part)
+    hidden, grad_gate_all, grad_up_all, _ = tie(hidden, grad_gate_all, grad_up_all, ffn_part)
+    hidden_all = gather_row(hidden, row_index)
     grad_down = jnp.einsum(
         "tf,td->fd", hidden_all, grad_branch, preferred_element_type=jnp.float32
     )
-    grad_gu = jnp.einsum(
-        "td,tkf->kfd", gathered_ffn, grad_gate_up, preferred_element_type=jnp.float32
-    )
-    total_down = dp_total(grad_down)
-    total_gu = dp_total(grad_gu.reshape(-1, row_width))
+    ffn_group = jnp.concatenate(
+        [
+            jnp.einsum("tf,td->fd", grad_gate_all, gathered_ffn, preferred_element_type=jnp.float32),
+            jnp.einsum("tf,td->fd", grad_up_all, gathered_ffn, preferred_element_type=jnp.float32),
+            grad_down,
+        ],
+        0,
+    ).astype(jnp.bfloat16)
+    grad_normed_ffn, ffn_group = tie(grad_normed_ffn, ffn_group)
+    total_ffn = dp_total(ffn_group)
+    hidden_units = w_down.shape[1]
+    total_gu = total_ffn[: 2 * hidden_units]
+    total_down = total_ffn[2 * hidden_units :]
 
     grad_middle, grad_gain_ffn = norm_backward(
         grad_normed_ffn, scaled_ffn, inverse_ffn, norm_ffn[0], model_width
     )
     grad_middle = cotangent.astype(jnp.float32) + grad_middle
     grad_middle_all = gather_tokens(grad_middle.astype(jnp.bfloat16))
-    grad_mixed = lax.psum_scatter(
-        jnp.einsum(
-            "td,hvd->htv", grad_middle_all, w_out[0], preferred_element_type=jnp.float32
-        ).astype(jnp.bfloat16),
-        "row",
-        scatter_dimension=0,
-        tiled=True,
+    grad_mixed = scatter_row(
+        lambda index: jnp.einsum(
+            "td,hvd->htv", grad_middle_all, own_half(w_out[0], index),
+            preferred_element_type=jnp.float32,
+        ),
+        row_index,
     )
     hidden_late, grad_mixed = tie(hidden_all, grad_mixed)
     last_branch = scatter_tokens(
@@ -537,19 +597,30 @@
         "htv,td->hvd", gathered_heads, grad_middle_all, preferred_element_type=jnp.float32
     )
     value_width = grad_out.shape[1]
-    total_out = dp_total(grad_out.reshape(-1, row_width))
-
     backs = [
         head_backward(head_args[head], head_kept[head], grad_mixed[head])
         for head in range(heads_dev)
     ]
     grad_proj_mine = jnp.stack([back[0] for back in backs], 0)
     grad_small_mine = jnp.stack([back[1] for back in backs], 0).astype(jnp.bfloat16)
-    grad_proj_all = gather_row(grad_proj_mine)
-    grad_small_all = gather_row(grad_small_mine)
-    grad_normed_in = scatter_tokens(
-        jnp.einsum("htp,dhp->td", grad_proj_all, w_proj[0], preferred_element_type=jnp.float32)
+    proj_came = swap_row(grad_proj_mine)
+    grad_small_all = gather_row(grad_small_mine, row_index)
+
+    def in_part(heads, index):
+        return jnp.einsum(
+            "htp,dhp->td", heads, own_half(w_proj[0], index, 1), preferred_element_type=jnp.float32
+        )
+
+    in_partial = (
+        in_part(grad_proj_mine, row_index)
+        + in_part(proj_came, 1 - row_index)
         + jnp.einsum("htp,dhp->td", grad_small_all, w_small[0], preferred_element_type=jnp.float32)
+    ).astype(jnp.bfloat16)
+    grad_normed_in = scatter_tokens(in_partial)
+    grad_proj_all = jnp.where(
+        row_index > 0,
+        jnp.concatenate([proj_came, grad_proj_mine], 0),
+        jnp.concatenate([grad_proj_mine, proj_came], 0),
     )
     grad_proj = jnp.einsum(
         "td,htp->hpd", gathered_in, grad_proj_all, preferred_element_type=jnp.float32
@@ -558,7 +629,13 @@
         "td,htp->hpd", gathered_in, grad_small_all, preferred_element_type=jnp.float32
     )
     proj_width = grad_proj.shape[1]
-    total_proj = dp_total(grad_proj.reshape(-1, row_width))
+    mixer_group = jnp.concatenate(
+        [grad_proj.reshape(-1, row_width), grad_out.reshape(-1, row_width)], 0
+    ).astype(jnp.bfloat16)
+    mixer_group, grad_small = tie(mixer_group, grad_small)
+    total_mixer = dp_total(mixer_group)
+    total_proj = total_mixer[: heads_col * proj_width]
+    total_out = total_mixer[heads_col * proj_width :]
     taps, channels = w_conv.shape[1], w_conv.shape[3]
     lanes = 128
 
@@ -570,38 +647,47 @@
         padded_lanes(jnp.stack([back[2] for back in backs], 1)),
         padded_lanes(jnp.stack([back[3].reshape(()) for back in backs])),
         padded_lanes(jnp.stack([back[4].reshape(()) for back in backs])),
+        padded_lanes(grad_small),
         padded_lanes(sum(back[5] for back in backs)),
         padded_lanes(grad_gain_ffn),
-        padded_lanes(grad_small),
     ]
     starts = [0]
     for piece in pieces:
         starts.append(starts[-1] + piece.shape[0])
-    summed = lax.psum(jnp.concatenate(pieces, 0), "dp")
-    shared = lax.all_gather(summed[: starts[5]], ("col", "row"), axis=0, tiled=False)
-    shared = shared.reshape(col_size, row_size, starts[5], lanes)
-    mine = lax.dynamic_index_in_dim(shared, col_index, 0, keepdims=False)
-
-    def taken(array, place, count):
-        flat = array[..., starts[place] : starts[place + 1], :]
-        return flat.reshape(flat.shape[:-2] + (-1,))[..., :count]
-
-    conv_rows = taken(mine, 0, taps * heads_dev * channels).reshape(
-        row_size, taps, heads_dev, channels
-    )
-    grad_conv = conv_rows.transpose(1, 0, 2, 3).reshape(1, taps, heads_col, channels)
-    grad_alog = taken(mine, 1, heads_dev).reshape(1, heads_col)
-    grad_bias = taken(mine, 2, heads_dev).reshape(1, heads_col)
-    grad_norm_out = taken(shared, 3, value_width).sum((0, 1))[None]
-    ffn_rows = taken(shared, 4, row_width).sum(0)
-    grad_norm_ffn = lax.dynamic_slice_in_dim(ffn_rows, row_index, 1, 0)
-    total_small = taken(summed, 5, grad_small.size).reshape(grad_small.shape)
+    summed = spread_total(jnp.concatenate(pieces, 0), "dp")
+    gains = spread_total(summed[starts[4] :], "col")
+    gain_rows = starts[5] - starts[4]
+    near = jnp.concatenate([summed[: starts[3]], gains[:gain_rows]], 0)
+    far = swap_row(near)
+
+    def taken(array, first, count):
+        return array[first:].reshape(-1)[:count]
+
+    def both(first, shape):
+        count = 1
+        for extent in shape:
+            count *= extent
+        mine = taken(near, first, count).reshape(shape)
+        other = taken(far, first, count).reshape(shape)
+        return jnp.where(
+            row_index > 0,
+            jnp.concatenate([other, mine], -1 if len(shape) == 1 else 1),
+            jnp.concatenate([mine, other], -1 if len(shape) == 1 else 1),
+        )[None]
+
+    grad_conv = both(starts[0], (taps, heads_dev, channels))
+    grad_alog = both(starts[1], (heads_dev,))
+    grad_bias = both(starts[2], (heads_dev,))
+    grad_norm_out = taken(near + far, starts[3], value_width)[None]
+    grad_norm_ffn = taken(gains, gain_rows, row_width)[None]
+    total_small = taken(summed, starts[3], grad_small.size).reshape(grad_small.shape)
 
     grad_in, grad_gain_in = norm_backward(
         grad_normed_in, scaled_in, inverse_in, norm_in[0], model_width
     )
     grad_rows = grad_middle + grad_in
-    grad_norm_in = lax.psum(grad_gain_in, ("dp", "col"))[None]
+    grad_norm_in = spread_total(spread_total(padded_lanes(grad_gain_in), "dp"), "col")
+    grad_norm_in = grad_norm_in.reshape(1, -1)[:, :row_width]
     return (
         result,
         grad_rows,

time: 536 us -> 396 us (0.74)
  waiting for transfers between devices: 232 us -> 155 us
  blocking collectives: 81.6 us -> 9.96 us
  local copies, waits for them, and re-layouts: 18.8 us -> 27.4 us
  other arithmetic: 47.5 us -> 41.3 us
    psum x2 -> x0, blocking collectives: 55.5 us -> none  [the longest x1 40 us: body(): grad_norm_in = lax.psum(grad_gain_in, ('dp', 'col'))[None]]
    reduce_scatter x5 -> x0, waiting for transfers between devices: 29.7 us -> none  [the longest x3 20.7 us: scatter_row(): lax.psum_scatter(partial_rows.astype(jnp.bfloat16), 'row', scatter_dimens...]
    all_gather x4 -> x0, waiting for transfers between devices: 23.5 us -> none  [gather_row(): return lax.all_gather(rows, 'row', axis=0, tiled=True)]
    ppermute x0 -> x24, starting transfers between devices: none -> 17.1 us  [the longest x12 15.4 us: spread_total(): lax.ppermute(array, axis_name, [(i, i ^ step * k) for i in range(size)])]
    all_gather x2 -> x0, blocking collectives: 16.1 us -> none  [the longest x1 13.9 us: body(): lax.all_gather(summed[:starts[5]], ('col', 'row'), axis=0, tiled=False)]
    reduce_scatter x4, waiting for transfers between devices: 56.8 us -> 41.2 us  [scatter_tokens(): lax.psum_scatter(partial_rows.astype(jnp.bfloat16), 'col', scatter_dimens...]
    ppermute x16 -> x8, waiting for transfers between devices: 26.6 us -> 13 us  [halving_total(): came = lax.ppermute(current, 'dp', [(i, i ^ bit) for i in range(size)])]
    ppermute x0 -> x24, waiting for transfers between devices: none -> 12 us  [the longest x12 8.45 us: swap_row(): return lax.ppermute(array, 'row', [(0, 1), (1, 0)])]
  transfers between devices with their start and end apart: 49 -> 48, of which waited for: 35 -> 23; matrix products, arithmetic and copies ran while one was open for 14% -> 22% of each run, Pallas kernels for 10% -> 14%
where the time goes in v2:
time: 396 us; the launch traced here: 390 us
  waiting for transfers between devices  155 us (39%)
  Pallas kernels  52.9 us (13%)
  matrix products  49.2 us (12%)
  other arithmetic  41.3 us (10%)
  starting transfers between devices  38.4 us (10%)
  local copies, waits for them, and re-layouts  27.4 us (7%)
  between operations  15.3 us (4%)
  blocking collectives  9.96 us (3%)
    all_gather x4, waiting for transfers between devices, gather_tokens(): return lax.all_gather(block_rows, 'col', axis=0, tiled=True)  75.4 us
    pallas_call x2, Pallas kernels, run_kernel(): pl.pallas_call(kernel, out_shape=out_shape, in_specs=[pl.BlockSpec(memory...  52.9 us
    reduce_scatter x4, waiting for transfers between devices, scatter_tokens(): lax.psum_scatter(partial_rows.astype(jnp.bfloat16), 'col', scatter_dimens...  41.2 us
    ppermute x12, starting transfers between devices, spread_total(): lax.ppermute(array, axis_name, [(i, i ^ step * k) for i in range(size)])  15.4 us
    ppermute x8, waiting for transfers between devices, halving_total(): came = lax.ppermute(away, 'dp', [(i, i ^ bit) for i in range(size)])  13.6 us
    ppermute x8, waiting for transfers between devices, halving_total(): came = lax.ppermute(current, 'dp', [(i, i ^ bit) for i in range(size)])  13 us
    ppermute x8, starting transfers between devices, halving_total(): came = lax.ppermute(away, 'dp', [(i, i ^ bit) for i in range(size)])  10.8 us
    psum x4, blocking collectives, row_total(): return lax.psum(partial_rows, 'row')  9.96 us
  transfers between devices with their start and end apart: 48, of which 23 were waited for; matrix products, arithmetic and copies ran while one was open for 22% of the time, Pallas kernels for 14%

profile of v2, /device:TPU:0, one launch (start us, length us, event | category | flops | bytes accessed | tf_op | source)
XLA Modules:
  0.0 389.7 jit_solution(6705425929928152042)
XLA Ops:
  8.4 2.6 psum.28
  12.8 6.8 %constant_dynamic-slice_fusion.6 = (bf16[1,512,1,768]{3,2,1,0:T(2,128)(2,1)}, bf16[1,512,1,768]{3,2,1,0:T(2,128)(2,1)}) fusion(bf16[1,512,2,768]{3,2,1,0:T(2,128)(2,1)} %param.16, s32[]{:T(128)S(6)} %select_n.242, s32[]{:T(128)S(6)} %select_n.243), kind=kLoop, calls=%fused_computation.166 | loop fusion | bytes 3145736 | tf_op jit(solution)/shard_map/dynamic_slice | solution.py:383
  19.6 23.8 %all-gather.5.cloned.1.call-done = bf16[1024,512]{1,0:T(8,128)(2,1)} async-done(((bf16[256,512]{1,0:T(8,128)(2,1)}), bf16[1024,512]{1,0:T(8,128)(2,1)}) %all-gather.5.cloned.1.call-update) | async-done | bytes 1048592 | tf_op jit(solution)/shard_map/all_gather | solution.py:368
  43.5 3.9 %fusion.11 = bf16[1,1024,768]{2,1,0:T(8,128)(2,1)} fusion(bf16[1024,512]{1,0:T(8,128)(2,1)} %all-gather.5.cloned.1.call-done, bf16[1,512,1,768]{3,2,1,0:T(2,128)(2,1)} %get-tuple-element.85), kind=kOutput, calls=%fused_computation.24 | convolution fusion | flops 806092800 | bytes 3407872 | tf_op jit(solution)/shard_map/td,dhp->htp/dot_general | solution.py:483
  52.4 4.5 %bitcast_add_fusion = f32[1,1024,768]{2,1,0:T(8,128)} fusion(bf16[1,1024,768]{2,1,0:T(8,128)(2,1)} %collective-permute-done, bf16[1024,512]{1,0:T(8,128)(2,1)S(1)} %copy-done.1, bf16[1,512,1,768]{3,2,1,0:T(2,128)(2,1)} %get-tuple-element.84), kind=kOutput, calls=%fused_computation.8 | convolution fusion | flops 806879232 | bytes 6553600 | tf_op jit(solution)/shard_map/td,dhp->htp/dot_general | solution.py:483
  57.3 24.9 %shard_map.237 = (bf16[1024,256]{1,0:T(8,128)(2,1)}, f32[1024,256]{1,0:T(8,128)}, f32[1024,256]{1,0:T(8,128)}, f32[2048,256]{1,0:T(8,128)}, f32[1024,256]{1,0:T(8,128)}) custom-call(f32[1024,768]{1,0:T(8,128)} %bitcast.189, f32[1024,2]{1,0:T(8,128)} %fusion.53.small_ref, f32[1024,1]{1,0:T(8,128)} %convert_element_type.249.reset_ref, f32[4,512]{1,0:T(4,128)} %bitcast.216, ...), custom_call_target="tpu_custom_call" | custom-call | flops 20000000000 | bytes 8000000 | tf_op jit(solution)/shard_map/pallas_call | solution.py:319
  82.2 2.4 all-gather.7.cloned.1.call-done
  90.5 2.4 collective-permute-done.3
  94.8 20.9 %reduce-scatter.5.cloned.1.call-done = bf16[256,512]{1,0:T(8,128)(2,1)} async-done(((bf16[1024,512]{1,0:T(8,128)(2,1)}), bf16[256,512]{1,0:T(8,128)(2,1)}) %reduce-scatter.5.cloned.1.call-update) | async-done | bytes 262160 | tf_op jit(solution)/shard_map/reduce_scatter | solution.py:372
  116.8 2.5 psum.29
  120.2 26.7 %all-gather.9.cloned.1.call-done = bf16[1024,512]{1,0:T(8,128)(2,1)} async-done(((bf16[256,512]{1,0:T(8,128)(2,1)}), bf16[1024,512]{1,0:T(8,128)(2,1)}) %all-gather.9.cloned.1.call-update) | async-done | bytes 1048592 | tf_op jit(solution)/shard_map/all_gather | solution.py:368
  146.9 2.6 fusion.12
  149.6 3.2 collective-permute-done.4
  153.8 2.0 multiply_convert_fusion
  156.3 2.0 collective-permute-done.6
  158.4 2.4 maximum_select_fusion.5
  160.7 2.1 fusion.34
  162.9 2.4 maximum_select_fusion.4
  166.4 2.0 add_convert_fusion
  168.7 2.7 convolution_convert_fusion.5
  174.9 20.3 %reduce-scatter.7.cloned.1.call-done = bf16[256,512]{1,0:T(8,128)(2,1)} async-done(((bf16[1024,512]{1,0:T(8,128)(2,1)}), bf16[256,512]{1,0:T(8,128)(2,1)}) %reduce-scatter.7.cloned.1.call-update) | async-done | bytes 262160 | tf_op jit(solution)/shard_map/reduce_scatter | solution.py:372
  197.3 2.5 psum.30
  199.8 2.0 fusion.91
  206.1 22.5 %all-gather.11.cloned.1.call-done = bf16[1024,512]{1,0:T(8,128)(2,1)} async-done(((bf16[256,512]{1,0:T(8,128)(2,1)}), bf16[1024,512]{1,0:T(8,128)(2,1)}) %all-gather.11.cloned.1.call-update) | async-done | bytes 1048592 | tf_op jit(solution)/shard_map/all_gather | solution.py:368
  230.5 2.7 convert_add_fusion.2
  236.2 27.9 %shard_map.238 = (bf16[1024,768]{1,0:T(8,128)(2,1)}, f32[1024,2]{1,0:T(8,128)}, f32[4,512]{1,0:T(4,128)}, f32[1,1]{1,0:T(1,128)}, f32[1,1]{1,0:T(1,128)}, /*index=5*/f32[1,256]{1,0:T(1,128)}) custom-call(f32[1024,768]{1,0:T(8,128)} %bitcast.190, f32[1024,2]{1,0:T(8,128)} %fusion.53.small_ref, f32[1024,1]{1,0:T(8,128)} %convert_element_type.249.reset_ref, ...), custom_call_target="tpu_custom_call" | custom-call | flops 40000000000 | bytes 8000000 | tf_op jit(solution)/shard_map/pallas_call | solution.py:319
  266.7 6.6 %collective-permute-done.37 = bf16[264,512]{1,0:T(8,128)(2,1)S(1)} collective-permute-done((bf16[264,512]{1,0:T(8,128)(2,1)S(1)}, bf16[264,512]{1,0:T(8,128)(2,1)S(1)}, u32[]{:S(2)}, u32[]{:S(2)}) %collective-permute-start.37) | collective-permute-done | bytes 270368 | tf_op jit(solution)/shard_map/ppermute | solution.py:441
  275.8 7.1 %collective-permute-done.38 = bf16[264,512]{1,0:T(8,128)(2,1)S(1)} collective-permute-done((bf16[264,512]{1,0:T(8,128)(2,1)S(1)}, bf16[264,512]{1,0:T(8,128)(2,1)S(1)}, u32[]{:S(2)}, u32[]{:S(2)}) %collective-permute-start.38) | collective-permute-done | bytes 270368 | tf_op jit(solution)/shard_map/ppermute | solution.py:446
  283.9 2.3 fusion.58
  286.5 3.3 fusion.9
  291.4 3.1 convolution_convert_fusion.8
  299.2 1.9 pad_maximum_fusion.1
  302.4 3.5 convolution_convert_fusion.2
  306.2 4.9 %fusion.8 = bf16[2,768,512]{2,1,0:T(8,128)(2,1)S(1)} fusion(bf16[1,1024,768]{2,1,0:T(8,128)(2,1)} %bitcast.224, bf16[1,1024,768]{2,1,0:T(8,128)(2,1)} %collective-permute-done.9, pred[]{:T(512)S(6)} %gt.6, bf16[1024,512]{1,0:T(8,128)(2,1)S(1)} %copy-done.2), kind=kOutput, calls=%fused_computation.17 | convolution fusion | flops 1616117760 | bytes 5767169 | tf_op jit(solution)/shard_map/td,htp->hpd/dot_general | solution.py:625
  311.9 2.1 collective-permute-start.27
  319.1 2.0 collective-permute-start.29
  321.2 1.8 collective-permute-start.30
  323.7 2.9 collective-permute-done.30
  335.0 4.2 %collective-permute-done.22 = bf16[256,512]{1,0:T(8,128)(2,1)S(1)} collective-permute-done((bf16[256,512]{1,0:T(8,128)(2,1)S(1)}, bf16[256,512]{1,0:T(8,128)(2,1)S(1)}, u32[]{:S(2)}, u32[]{:S(2)}) %collective-permute-start.22) | collective-permute-done | bytes 262176 | tf_op jit(solution)/shard_map/ppermute | solution.py:441
  343.0 1.9 broadcast_select_fusion.5
  348.0 2.1 collective-permute-start.20
  350.1 1.9 broadcast_select_fusion.6
  353.2 4.6 %collective-permute-done.24 = bf16[512,512]{1,0:T(8,128)(2,1)S(1)} collective-permute-done((bf16[512,512]{1,0:T(8,128)(2,1)S(1)}, bf16[512,512]{1,0:T(8,128)(2,1)S(1)}, u32[]{:S(2)}, u32[]{:S(2)}) %collective-permute-start.24) | collective-permute-done | bytes 524320 | tf_op jit(solution)/shard_map/ppermute | solution.py:446
  359.6 2.0 pad_maximum_fusion
  361.6 5.9 %copy.76 = f32[2,768,512]{1,0,2:T(2,128)} copy(f32[2,768,512]{2,1,0:T(8,128)} %bitcast.188) | data formatting | bytes 6291456 | tf_op jit(solution)/shard_map/reshape | solution.py:695
  372.2 2.4 psum.31
  375.3 1.9 collective-permute-start.16
  379.7 2.2 fusion.43
  (249 shorter events, 83.2 us)
Async XLA Ops:
  7.2 36.3 %all-gather.5.cloned.1.call-start = ((), (), s32[]{:S(2)}) async-start(), calls=%async_computation.4 | async-start | bytes 1310720 | tf_op jit(solution)/shard_map/all_gather | solution.py:368
  12.8 71.8 %all-gather.7.cloned.1.call-start = ((), (), s32[]{:S(2)}) async-start(), calls=%async_computation.5 | async-start | bytes 1310720 | tf_op jit(solution)/shard_map/all_gather | solution.py:368
  47.4 5.0 %collective-permute-start = (bf16[1,1024,768]{2,1,0:T(8,128)(2,1)}, bf16[1,1024,768]{2,1,0:T(8,128)(2,1)}, u32[]{:S(2)}, u32[]{:S(2)}) collective-permute-start(bf16[1,1024,768]{2,1,0:T(8,128)(2,1)} %fusion.11), channel_id=1, source_target_pairs={{0,4},{4,0},{1,5},{5,1},{2,6},{6,2},{3,7},{7,3},{8,12},{12,8},{9,1... | collective-permute-start | bytes 4718600 | tf_op jit(solution)/shard_map/ppermute | solution.py:378
  48.1 3.5 collective-permute-start.1
  57.0 58.7 %reduce-scatter.5.cloned.1.call-start = ((), (), s32[]{:S(2)}) async-start(), calls=%async_computation.6 | async-start | bytes 1310720 | tf_op jit(solution)/shard_map/reduce_scatter | solution.py:372
  84.6 2.1 collective-permute-start.2
  88.9 58.0 %all-gather.9.cloned.1.call-start = ((), (), s32[]{:S(2)}) async-start(), calls=%async_computation.7 | async-start | bytes 1310720 | tf_op jit(solution)/shard_map/all_gather | solution.py:368
  90.4 2.5 collective-permute-start.3
  120.2 75.1 %reduce-scatter.7.cloned.1.call-start = ((), (), s32[]{:S(2)}) async-start(), calls=%async_computation.8 | async-start | bytes 1310720 | tf_op jit(solution)/shard_map/reduce_scatter | solution.py:372
  149.5 3.3 collective-permute-start.4
  155.8 2.5 collective-permute-start.6
  156.0 6.9 %collective-permute-start.5 = (bf16[512,704]{0,1:T(8,128)(2,1)}, bf16[512,704]{0,1:T(8,128)(2,1)}, u32[]{:S(2)}, u32[]{:S(2)}) collective-permute-start(bf16[512,704]{0,1:T(8,128)(2,1)} %get-tuple-element.74), channel_id=1, source_target_pairs={{0,4},{4,0},{1,5},{5,1},{2,6},{6,2},{3,7},{7,3},{8,12},{12,8},{9,1... | collective-permute-start | bytes 2162696 | tf_op jit(solution)/shard_map/ppermute | solution.py:378
  168.4 60.1 %all-gather.11.cloned.1.call-start = ((), (), s32[]{:S(2)}) async-start(), calls=%async_computation.9 | async-start | bytes 1310720 | tf_op jit(solution)/shard_map/all_gather | solution.py:368
  168.5 3.8 collective-permute-start.7
  201.8 165.6 %reduce-scatter.11.cloned.1.call-start = ((), (), s32[]{:S(2)}) async-start(), calls=%async_computation.11 | async-start | bytes 1310720 | tf_op jit(solution)/shard_map/reduce_scatter | solution.py:372
  203.1 27.3 %collective-permute-start.32 = (bf16[528,512]{1,0:T(8,128)(2,1)}, bf16[528,512]{1,0:T(8,128)(2,1)}, u32[]{:S(2)}, u32[]{:S(2)}) collective-permute-start(bf16[528,512]{1,0:T(8,128)(2,1)} %get-tuple-element.78), channel_id=1, source_target_pairs={{0,8},{8,0},{16,24},{24,16},{1,9},{9,1},{17,25},{25,17},{2,10},{10... | collective-permute-start | bytes 1622024 | tf_op jit(solution)/shard_map/ppermute | solution.py:441
  204.6 25.9 %collective-permute-start.36 = (bf16[528,512]{1,0:T(8,128)(2,1)}, bf16[528,512]{1,0:T(8,128)(2,1)}, u32[]{:S(2)}, u32[]{:S(2)}) collective-permute-start(bf16[528,512]{1,0:T(8,128)(2,1)} %get-tuple-element.79), channel_id=1, source_target_pairs={{0,16},{8,24},{16,0},{24,8},{1,17},{9,25},{17,1},{25,9},{2,18},{10... | collective-permute-start | bytes 1622024 | tf_op jit(solution)/shard_map/ppermute | solution.py:441
  230.4 4.4 %collective-permute-start.8 = (bf16[1,1024,256]{2,1,0:T(8,128)(2,1)S(1)}, bf16[1,1024,256]{2,1,0:T(8,128)(2,1)S(1)}, u32[]{:S(2)}, u32[]{:S(2)}) collective-permute-start(bf16[1,1024,256]{2,1,0:T(8,128)(2,1)S(1)} %fusion.13), channel_id=1, source_target_pairs={{0,4},{4,0},{1,5},{5,1},{2,6},{6,2},{3,7},{7,3},{8,12},{12,8},{9,1... | collective-permute-start | bytes 1572872 | tf_op jit(solution)/shard_map/ppermute | solution.py:378
  233.2 32.7 %collective-permute-start.33 = (bf16[264,512]{1,0:T(8,128)(2,1)S(1)}, bf16[264,512]{1,0:T(8,128)(2,1)S(1)}, u32[]{:S(2)}, u32[]{:S(2)}) collective-permute-start(bf16[264,512]{1,0:T(8,128)(2,1)S(1)} %select_convert_fusion.1), channel_id=1, source_target_pairs={{0,16},{8,24},{16,0},{24,8},{1,17},{9,25},{17,1},{25,9},{2,18},{10... | collective-permute-start | bytes 811016 | tf_op jit(solution)/shard_map/ppermute | solution.py:441
  264.2 22.3 %collective-permute-start.9 = (bf16[1,1024,768]{2,1,0:T(8,128)(2,1)}, bf16[1,1024,768]{2,1,0:T(8,128)(2,1)}, u32[]{:S(2)}, u32[]{:S(2)}) collective-permute-start(bf16[1,1024,768]{2,1,0:T(8,128)(2,1)} %bitcast.223), channel_id=1, source_target_pairs={{0,4},{4,0},{1,5},{5,1},{2,6},{6,2},{3,7},{7,3},{8,12},{12,8},{9,1... | collective-permute-start | bytes 4718600 | tf_op jit(solution)/shard_map/ppermute | solution.py:378
  264.4 8.9 %collective-permute-start.37 = (bf16[264,512]{1,0:T(8,128)(2,1)S(1)}, bf16[264,512]{1,0:T(8,128)(2,1)S(1)}, u32[]{:S(2)}, u32[]{:S(2)}) collective-permute-start(bf16[264,512]{1,0:T(8,128)(2,1)S(1)} %select_convert_fusion), channel_id=1, source_target_pairs={{0,8},{8,0},{16,24},{24,16},{1,9},{9,1},{17,25},{25,17},{2,10},{10... | collective-permute-start | bytes 811016 | tf_op jit(solution)/shard_map/ppermute | solution.py:441
  266.1 8.9 %collective-permute-start.34 = (bf16[264,512]{1,0:T(8,128)(2,1)S(1)}, bf16[264,512]{1,0:T(8,128)(2,1)S(1)}, u32[]{:S(2)}, u32[]{:S(2)}) collective-permute-start(bf16[264,512]{1,0:T(8,128)(2,1)S(1)} %add_convert_fusion.2), channel_id=1, source_target_pairs={{0,16},{8,24},{16,0},{24,8},{1,17},{9,25},{17,1},{25,9},{2,18},{10... | collective-permute-start | bytes 811016 | tf_op jit(solution)/shard_map/ppermute | solution.py:446
  273.4 9.5 %collective-permute-start.38 = (bf16[264,512]{1,0:T(8,128)(2,1)S(1)}, bf16[264,512]{1,0:T(8,128)(2,1)S(1)}, u32[]{:S(2)}, u32[]{:S(2)}) collective-permute-start(bf16[264,512]{1,0:T(8,128)(2,1)S(1)} %add_convert_fusion.1), channel_id=1, source_target_pairs={{0,8},{8,0},{16,24},{24,16},{1,9},{9,1},{17,25},{25,17},{2,10},{10... | collective-permute-start | bytes 811016 | tf_op jit(solution)/shard_map/ppermute | solution.py:446
  275.2 22.4 %collective-permute-start.35 = (bf16[528,512]{1,0:T(8,128)(2,1)S(1)}, bf16[528,512]{1,0:T(8,128)(2,1)}, u32[]{:S(2)}, u32[]{:S(2)}) collective-permute-start(bf16[528,512]{1,0:T(8,128)(2,1)S(1)} %maximum_select_fusion.13), channel_id=1, source_target_pairs={{0,8},{8,0},{16,24},{24,16},{1,9},{9,1},{17,25},{25,17},{2,10},{10... | collective-permute-start | bytes 1622024 | tf_op jit(solution)/shard_map/ppermute | solution.py:446
  283.1 11.8 %collective-permute-start.39 = (bf16[528,512]{1,0:T(8,128)(2,1)S(1)}, bf16[528,512]{1,0:T(8,128)(2,1)}, u32[]{:S(2)}, u32[]{:S(2)}) collective-permute-start(bf16[528,512]{1,0:T(8,128)(2,1)S(1)} %maximum_select_fusion.14), channel_id=1, source_target_pairs={{0,16},{8,24},{16,0},{24,8},{1,17},{9,25},{17,1},{25,9},{2,18},{10... | collective-permute-start | bytes 1622024 | tf_op jit(solution)/shard_map/ppermute | solution.py:446
  283.8 2.6 collective-permute-start.10
  291.4 88.3 %reduce-scatter.9.cloned.1.call-start = ((), (), s32[]{:S(2)}) async-start(), calls=%async_computation.10 | async-start | bytes 1310720 | tf_op jit(solution)/shard_map/reduce_scatter | solution.py:372
  311.9 7.2 %collective-permute-start.27 = (f32[40,128]{1,0:T(8,128)S(1)}, f32[40,128]{1,0:T(8,128)S(1)}, u32[]{:S(2)}, u32[]{:S(2)}) collective-permute-start(f32[40,128]{1,0:T(8,128)S(1)} %concatenate.199), channel_id=1, source_target_pairs={{0,24},{8,16},{16,8},{24,0},{1,25},{9,17},{17,9},{25,1},{2,26},{10... | collective-permute-start | bytes 61448 | tf_op jit(solution)/shard_map/ppermute | solution.py:404
  314.0 5.1 %collective-permute-start.26 = (f32[40,128]{1,0:T(8,128)S(1)}, f32[40,128]{1,0:T(8,128)S(1)}, u32[]{:S(2)}, u32[]{:S(2)}) collective-permute-start(f32[40,128]{1,0:T(8,128)S(1)} %concatenate.199), channel_id=1, source_target_pairs={{0,16},{8,24},{16,0},{24,8},{1,17},{9,25},{17,1},{25,9},{2,18},{10... | collective-permute-start | bytes 61448 | tf_op jit(solution)/shard_map/ppermute | solution.py:404
  314.8 4.3 %collective-permute-start.25 = (f32[40,128]{1,0:T(8,128)S(1)}, f32[40,128]{1,0:T(8,128)S(1)}, u32[]{:S(2)}, u32[]{:S(2)}) collective-permute-start(f32[40,128]{1,0:T(8,128)S(1)} %concatenate.199), channel_id=1, source_target_pairs={{0,8},{8,0},{16,24},{24,16},{1,9},{9,1},{17,25},{25,17},{2,10},{10... | collective-permute-start | bytes 61448 | tf_op jit(solution)/shard_map/ppermute | solution.py:404
  316.5 13.4 %collective-permute-start.17 = (bf16[512,512]{1,0:T(8,128)(2,1)}, bf16[512,512]{1,0:T(8,128)(2,1)}, u32[]{:S(2)}, u32[]{:S(2)}) collective-permute-start(bf16[512,512]{1,0:T(8,128)(2,1)} %get-tuple-element.82), channel_id=1, source_target_pairs={{0,8},{8,0},{16,24},{24,16},{1,9},{9,1},{17,25},{25,17},{2,10},{10... | collective-permute-start | bytes 1572872 | tf_op jit(solution)/shard_map/ppermute | solution.py:441
  317.9 13.2 %collective-permute-start.21 = (bf16[512,512]{1,0:T(8,128)(2,1)}, bf16[512,512]{1,0:T(8,128)(2,1)}, u32[]{:S(2)}, u32[]{:S(2)}) collective-permute-start(bf16[512,512]{1,0:T(8,128)(2,1)} %get-tuple-element.83), channel_id=1, source_target_pairs={{0,16},{8,24},{16,0},{24,8},{1,17},{9,25},{17,1},{25,9},{2,18},{10... | collective-permute-start | bytes 1572872 | tf_op jit(solution)/shard_map/ppermute | solution.py:441
  319.1 4.6 %collective-permute-start.29 = (f32[6,128]{1,0:T(8,128)S(1)}, f32[6,128]{1,0:T(8,128)S(1)}, u32[]{:S(2)}, u32[]{:S(2)}) collective-permute-start(f32[6,128]{1,0:T(8,128)S(1)} %slice.189), channel_id=1, source_target_pairs={{0,2},{1,3},{2,0},{3,1},{4,6},{5,7},{6,4},{7,5},{8,10},{9,11},{10,... | collective-permute-start | bytes 9224 | tf_op jit(solution)/shard_map/ppermute | solution.py:404
  321.2 5.4 %collective-permute-start.30 = (f32[6,128]{1,0:T(8,128)S(1)}, f32[6,128]{1,0:T(8,128)S(1)}, u32[]{:S(2)}, u32[]{:S(2)}) collective-permute-start(f32[6,128]{1,0:T(8,128)S(1)} %slice.189), channel_id=1, source_target_pairs={{0,3},{1,2},{2,1},{3,0},{4,7},{5,6},{6,5},{7,4},{8,11},{9,10},{10,... | collective-permute-start | bytes 9224 | tf_op jit(solution)/shard_map/ppermute | solution.py:404
  323.0 3.6 collective-permute-start.28
  328.3 6.7 %collective-permute-start.31 = (f32[20,128]{1,0:T(8,128)S(1)}, f32[20,128]{1,0:T(8,128)S(1)}, u32[]{:S(2)}, u32[]{:S(2)}) collective-permute-start(f32[20,128]{1,0:T(8,128)S(1)} %pad_maximum_fusion.4), channel_id=1, source_target_pairs={{0,4},{4,0},{1,5},{5,1},{2,6},{6,2},{3,7},{7,3},{8,12},{12,8},{9,1... | collective-permute-start | bytes 30728 | tf_op jit(solution)/shard_map/ppermute | solution.py:378
  332.8 6.4 %collective-permute-start.22 = (bf16[256,512]{1,0:T(8,128)(2,1)S(1)}, bf16[256,512]{1,0:T(8,128)(2,1)S(1)}, u32[]{:S(2)}, u32[]{:S(2)}) collective-permute-start(bf16[256,512]{1,0:T(8,128)(2,1)S(1)} %select_convert_fusion.2), channel_id=1, source_target_pairs={{0,8},{8,0},{16,24},{24,16},{1,9},{9,1},{17,25},{25,17},{2,10},{10... | collective-permute-start | bytes 786440 | tf_op jit(solution)/shard_map/ppermute | solution.py:441
  333.5 6.5 %collective-permute-start.18 = (bf16[256,512]{1,0:T(8,128)(2,1)S(1)}, bf16[256,512]{1,0:T(8,128)(2,1)S(1)}, u32[]{:S(2)}, u32[]{:S(2)}) collective-permute-start(bf16[256,512]{1,0:T(8,128)(2,1)S(1)} %select_convert_fusion.3), channel_id=1, source_target_pairs={{0,16},{8,24},{16,0},{24,8},{1,17},{9,25},{17,1},{25,9},{2,18},{10... | collective-permute-start | bytes 786440 | tf_op jit(solution)/shard_map/ppermute | solution.py:441
  339.4 6.4 %collective-permute-start.23 = (bf16[256,512]{1,0:T(8,128)(2,1)S(1)}, bf16[256,512]{1,0:T(8,128)(2,1)S(1)}, u32[]{:S(2)}, u32[]{:S(2)}) collective-permute-start(bf16[256,512]{1,0:T(8,128)(2,1)S(1)} %add_convert_fusion.3), channel_id=1, source_target_pairs={{0,8},{8,0},{16,24},{24,16},{1,9},{9,1},{17,25},{25,17},{2,10},{10... | collective-permute-start | bytes 786440 | tf_op jit(solution)/shard_map/ppermute | solution.py:446
  340.1 7.7 %collective-permute-start.19 = (bf16[256,512]{1,0:T(8,128)(2,1)S(1)}, bf16[256,512]{1,0:T(8,128)(2,1)S(1)}, u32[]{:S(2)}, u32[]{:S(2)}) collective-permute-start(bf16[256,512]{1,0:T(8,128)(2,1)S(1)} %add_convert_fusion.4), channel_id=1, source_target_pairs={{0,16},{8,24},{16,0},{24,8},{1,17},{9,25},{17,1},{25,9},{2,18},{10... | collective-permute-start | bytes 786440 | tf_op jit(solution)/shard_map/ppermute | solution.py:446
  346.0 11.8 %collective-permute-start.24 = (bf16[512,512]{1,0:T(8,128)(2,1)S(1)}, bf16[512,512]{1,0:T(8,128)(2,1)S(1)}, u32[]{:S(2)}, u32[]{:S(2)}) collective-permute-start(bf16[512,512]{1,0:T(8,128)(2,1)S(1)} %maximum_select_fusion.16), channel_id=1, source_target_pairs={{0,16},{8,24},{16,0},{24,8},{1,17},{9,25},{17,1},{25,9},{2,18},{10... | collective-permute-start | bytes 1572872 | tf_op jit(solution)/shard_map/ppermute | solution.py:446
  348.0 11.2 %collective-permute-start.20 = (bf16[512,512]{1,0:T(8,128)(2,1)S(1)}, bf16[512,512]{1,0:T(8,128)(2,1)S(1)}, u32[]{:S(2)}, u32[]{:S(2)}) collective-permute-start(bf16[512,512]{1,0:T(8,128)(2,1)S(1)} %maximum_select_fusion.15), channel_id=1, source_target_pairs={{0,8},{8,0},{16,24},{24,16},{1,9},{9,1},{17,25},{25,17},{2,10},{10... | collective-permute-start | bytes 1572872 | tf_op jit(solution)/shard_map/ppermute | solution.py:446
  368.7 6.0 %collective-permute-start.12 = (f32[4,128]{1,0:T(4,128)S(1)}, f32[4,128]{1,0:T(4,128)S(1)}, u32[]{:S(2)}, u32[]{:S(2)}) collective-permute-start(f32[4,128]{1,0:T(4,128)S(1)} %bitcast.213), channel_id=1, source_target_pairs={{0,16},{8,24},{16,0},{24,8},{1,17},{9,25},{17,1},{25,9},{2,18},{10... | collective-permute-start | bytes 6152 | tf_op jit(solution)/shard_map/ppermute | solution.py:404
  370.5 4.5 %collective-permute-start.13 = (f32[4,128]{1,0:T(4,128)S(1)}, f32[4,128]{1,0:T(4,128)S(1)}, u32[]{:S(2)}, u32[]{:S(2)}) collective-permute-start(f32[4,128]{1,0:T(4,128)S(1)} %bitcast.214), channel_id=1, source_target_pairs={{0,24},{8,16},{16,8},{24,0},{1,25},{9,17},{17,9},{25,1},{2,26},{10... | collective-permute-start | bytes 6152 | tf_op jit(solution)/shard_map/ppermute | solution.py:404
  371.7 3.6 collective-permute-start.11
  375.3 6.6 %collective-permute-start.16 = (f32[4,128]{1,0:T(4,128)S(1)}, f32[4,128]{1,0:T(4,128)S(1)}, u32[]{:S(2)}, u32[]{:S(2)}) collective-permute-start(f32[4,128]{1,0:T(4,128)S(1)} %add_add_fusion.3), channel_id=1, source_target_pairs={{0,3},{1,2},{2,1},{3,0},{4,7},{5,6},{6,5},{7,4},{8,11},{9,10},{10,... | collective-permute-start | bytes 6152 | tf_op jit(solution)/shard_map/ppermute | solution.py:404
  377.2 4.7 %collective-permute-start.15 = (f32[4,128]{1,0:T(4,128)S(1)}, f32[4,128]{1,0:T(4,128)S(1)}, u32[]{:S(2)}, u32[]{:S(2)}) collective-permute-start(f32[4,128]{1,0:T(4,128)S(1)} %add_add_fusion.3), channel_id=1, source_target_pairs={{0,2},{1,3},{2,0},{3,1},{4,6},{5,7},{6,4},{7,5},{8,10},{9,11},{10,... | collective-permute-start | bytes 6152 | tf_op jit(solution)/shard_map/ppermute | solution.py:404
  378.2 3.7 collective-permute-start.14
  (38 other events, 378.1 us)
Sparse Core Ops, SparseCore 0:
  12.9 30.5 all-gather.4
  57.1 27.4 all-gather.6
  89.0 26.5 reduce-scatter.4
  120.3 26.5 all-gather.8
  168.6 26.6 reduce-scatter.6
  201.9 26.5 all-gather.10
  291.5 26.7 reduce-scatter.10
  320.7 25.8 reduce-scatter.8
